TPU v7x, 128 devices: a whole 4x4x4 slice. The times are simulated.
128 devices in a mesh: section: 16 (over z_hi, y, core), slab: 8 (over x, z_lo).
Axes of the slice: x: 4, y: 4, z: 4 (z_hi: 2, z_lo: 2; z = z_hi * 2 + z_lo), core: 2. Of those that a mesh axis runs over, the one named last changes fastest.
Arguments:
- emitted: bfloat16 [16, 20, 512, 512], P('section', None, 'slab'), may hold values from -6 to 6
- returned: bfloat16 [16, 20, 512, 512], P('section', None, 'slab'), may hold values from -6 to 6
- stash: bfloat16 [16, 20, 512, 512], P('section', None, 'slab'), may hold values from -6 to 6
- skip_w: bfloat16 [16, 2, 20, 20], P('section'), may hold values from -1.25 to 1.25
- up_w: bfloat16 [16, 2, 80, 20], P('section'), may hold values from -1.25 to 1.25
- down_w: bfloat16 [16, 2, 20, 80], P('section'), may hold values from -0.625 to 0.625
- spec_w: bfloat16 [16, 2, 64, 2, 20, 20, 128], P('section', None, 'slab'), may hold values from -4 to 4
Outputs:
- sent: bfloat16 [16, 20, 512, 512], P('section', None, 'slab')
- back_grad: bfloat16 [16, 20, 512, 512], P('section', None, 'slab')
- grad_skip: float32 [16, 2, 20, 20], P('section')
- grad_up: float32 [16, 2, 80, 20], P('section')
- grad_down: float32 [16, 2, 20, 80], P('section')
- grad_spec: float32 [16, 2, 64, 2, 20, 20, 128], P('section', None, 'slab')
All inputs are finite; a program needn't handle non-finite values.
Results may differ from a plain program's by a relative error of at most 0.03.
Values may be sent and summed in bfloat16 or wider, within the bound.
No kernel may reach another device: no remote copies, remote signals or barrier semaphores. Data moves between devices by JAX's collectives and lax.ppermute only.
A program may use at most 192 MiB of HBM per device.

v0:
```python
import functools

import jax
import jax.numpy as jnp
import numpy as np
import ml_dtypes
from jax import lax
from jax.experimental import pallas as pl
from jax.experimental.pallas import tpu as pltpu
from jax.sharding import PartitionSpec as P

M = 64
LAYERS = 2
N = 512
C = 20
F = 80
SLABS = 8
ROWS = N // SLABS
KB = M // SLABS
CP = C // 2
EARLY = CP // 2
WIRE = C * KB
LANES = 128
BF = jnp.bfloat16
F32 = jnp.float32

root_two_pi = 0.7978845608028654
cubic_coef = 0.044715


def np_angles(left_idx, right_idx, length):
    product_idx = left_idx[:, None] * right_idx[None, :] % length
    return np.float32(2.0 * np.pi / length) * product_idx.astype(np.float32)


def np_tables():
    cell = np.arange(N)
    low = np.arange(M)
    both = np.concatenate([low, low + (N - M)])
    along_w = np_angles(cell, low, N)
    cos_w, sin_w = np.cos(along_w), np.sin(along_w)
    row = np.stack([cos_w.T, -sin_w.T], 0)
    weight = np.where(low == 0, 1.0, 2.0).astype(np.float32)[None, :, None]
    back = row * weight
    along_h = np_angles(cell, both, N)
    cos_h, sin_h = np.cos(along_h), np.sin(along_h)
    col = np.stack([np.stack([cos_h, -sin_h], 1), np.stack([sin_h, cos_h], 1)], 0)
    col = col.reshape(2, SLABS, ROWS, 2, 2 * M).transpose(1, 0, 2, 3, 4).reshape(SLABS, 2 * ROWS, 4 * M)

    def forward(table, scale):
        t = table.reshape(2, SLABS, KB, N).transpose(1, 0, 2, 3).reshape(2 * M, N)
        return (t.astype(ml_dtypes.bfloat16).astype(np.float32) * scale).astype(ml_dtypes.bfloat16)

    def inverse(table, scale):
        t = table.reshape(2, SLABS, KB, N)
        out = np.zeros((2, 2, SLABS, 2, KB, N), np.float32)
        for c in range(2):
            out[c, :, :, c] = t
        out = out.reshape(2, 4 * M, N)
        return (out.astype(ml_dtypes.bfloat16).astype(np.float32) * scale).astype(ml_dtypes.bfloat16)

    return {
        "ew": forward(row, 1.0),
        "ei": forward(back, 1.0 / N),
        "ewz": inverse(row, 1.0),
        "eiz": inverse(back, 1.0 / N),
        "col": col.astype(ml_dtypes.bfloat16),
    }


def dot(a, b):
    return jnp.dot(a, b, preferred_element_type=F32)


def dot_nt(a, b):
    return lax.dot_general(a, b, (((1,), (1,)), ((), ())), preferred_element_type=F32)


def gate(t):
    t = t.astype(BF)
    u = t * (BF(root_two_pi) + BF(root_two_pi * cubic_coef) * (t * t))
    half = BF(0.5) * t
    return half + half * jnp.tanh(u)


def gate_and_slope(t):
    t = t.astype(BF)
    tt = t * t
    th = jnp.tanh(t * (BF(root_two_pi) + BF(root_two_pi * cubic_coef) * tt))
    half = BF(0.5) * t
    value = half + half * th
    slope = (BF(0.5) + BF(0.5) * th) + half * (BF(1.0) - th * th) * (
        BF(root_two_pi) + BF(3.0 * root_two_pi * cubic_coef) * tt
    )
    return value, slope


def rows_to_wire(read, table_ref, send_ref):
    lane = lax.broadcasted_iota(jnp.int32, (M, LANES), 1)
    low = lane < ROWS
    table = table_ref[...]
    for cp in range(0, CP, 2):
        res = dot_nt(table, read(cp, 2))
        for s in range(2):
            r = res[:, s * LANES : (s + 1) * LANES].reshape(SLABS, 2, KB, LANES)
            a = r[:, 0].reshape(M, LANES)
            b = r[:, 1].reshape(M, LANES)
            lo = jnp.where(low, a, pltpu.roll(b, ROWS, 1)).reshape(SLABS, 1, KB, LANES)
            hi = jnp.where(low, pltpu.roll(a, ROWS, 1), b).reshape(SLABS, 1, KB, LANES)
            out = jnp.concatenate([lo, hi], axis=1).reshape(SLABS, 2 * KB, LANES).astype(BF)
            at = (cp + s) * 2 * KB
            send_ref[:, at : at + 2 * KB, :] = out


def wire_to_rows(recv_ref, left_ref):
    for cp in range(CP):
        m = recv_ref[:, cp * 2 * KB : (cp + 1) * 2 * KB, :].reshape(2 * M, LANES)
        t = m.astype(F32).T.astype(BF)
        left_ref[cp * ROWS : (cp + 1) * ROWS, 0 : 2 * M] = t[:ROWS]
        left_ref[cp * ROWS : (cp + 1) * ROWS, 2 * M : 4 * M] = t[ROWS:]


def wide(block):
    x = block.astype(F32)
    return jnp.concatenate([x[:, :, s * 8 : s * 8 + 8, :].reshape(8 * C, N) for s in range(2)], axis=1)


def narrow(x):
    parts = [x[:, s * N : (s + 1) * N].reshape(CP, 2, 8, N) for s in range(2)]
    return jnp.concatenate(parts, axis=2).astype(BF)


def field_read(ref):
    def read(cp, pairs):
        return ref[cp : cp + pairs].reshape(pairs * 2 * ROWS, N)

    return read


def row_dft_body(v_ref, table_ref, *rest):
    send_ref = rest[-1]
    rows_to_wire(field_read(v_ref), table_ref, send_ref)


def forward_body(keep, last, *refs):
    u_ref, v_ref, ws_ref, w1_ref, w2_ref, eiz_ref, ew_ref = refs[:7]
    outs = list(refs[7:])
    left_ref, z_ref = outs[-2:]
    outs = outs[:-2]
    out_ref = outs[0]
    at = 1
    if not last:
        send_ref = outs[at]
        at += 1
    if keep:
        y_ref, slope_ref = outs[at : at + 2]
    wire_to_rows(u_ref, left_ref)
    for c2 in range(2):
        z_ref[:, c2] = dot(left_ref[...], eiz_ref[c2]).reshape(CP, ROWS, N)

    def step(i, carry):
        h0 = pl.multiple_of(i * 16, 16)
        where = (slice(None), slice(None), pl.ds(h0, 16))
        v = wide(v_ref[where])
        z = wide(z_ref[where]) + dot(ws_ref[...], v.astype(BF))
        if keep:
            y, slope = gate_and_slope(z)
            y_ref[where] = narrow(y.astype(F32))
            slope_ref[where] = narrow(slope.astype(F32))
        else:
            y = gate(z)
        hidden = dot(w1_ref[...], y.astype(BF))
        out_ref[where] = narrow(v + dot(w2_ref[...], gate(hidden)))
        return carry

    lax.fori_loop(0, ROWS // 16, step, 0)
    if not last:
        rows_to_wire(field_read(out_ref), ew_ref, send_ref)


def back_body(first, layer, *refs):
    refs = list(refs)
    u_ref, table_ref, v_ref, wst_ref, w1_ref, w1t_ref, w2t_ref, ei_ref = refs[:8]
    if first:
        g_ref, ws_ref = refs[8:10]
        refs = refs[10:]
    else:
        base_in_ref, grads_in_ref, y_ref, slope_ref = refs[8:12]
        refs = refs[12:]
    base_ref, send_ref, grads_ref, gz_ref, gd_ref, gu_ref, gs_ref, left_ref, field_ref = refs
    wire_to_rows(u_ref, left_ref)
    for c2 in range(2):
        r = dot(left_ref[...], table_ref[c2]).reshape(CP, ROWS, N)
        if not first:
            r = (base_in_ref[:, c2].astype(F32) + r).astype(BF)
        field_ref[:, c2] = r
    if not first:
        g_ref = field_ref
    gd_ref[...] = jnp.zeros_like(gd_ref)
    gu_ref[...] = jnp.zeros_like(gu_ref)
    gs_ref[...] = jnp.zeros_like(gs_ref)

    def step(i, carry):
        h0 = pl.multiple_of(i * 16, 16)
        where = (slice(None), slice(None), pl.ds(h0, 16))
        g = wide(g_ref[where])
        gb = g.astype(BF)
        v = wide(v_ref[where]).astype(BF)
        if first:
            y, out_slope = gate_and_slope(wide(field_ref[where]) + dot(ws_ref[...], v))
            out_slope = out_slope.astype(F32)
        else:
            y = wide(y_ref[where]).astype(BF)
            out_slope = wide(slope_ref[where])
        act, slope = gate_and_slope(dot(w1_ref[...], y))
        gh = dot(w2t_ref[...], gb).astype(BF) * slope
        gz = (dot(w1t_ref[...], gh) * out_slope).astype(BF)
        base_ref[where] = narrow(g + dot(wst_ref[...], gz))
        gz_ref[where] = narrow(gz.astype(F32))
        gd_ref[...] += dot_nt(act.astype(BF), gb)
        gu_ref[...] += dot_nt(gh, y)
        gs_ref[...] += dot_nt(gz, v)
        return carry

    lax.fori_loop(0, ROWS // 16, step, 0)
    rows_to_wire(field_read(gz_ref), ei_ref, send_ref)
    total = jnp.zeros((F, LANES), F32) if first else grads_in_ref[...]
    for ref, slot in ((gd_ref, 0), (gu_ref, 1), (gs_ref, 2)):
        rows, cols = ref.shape
        r_idx = lax.broadcasted_iota(jnp.int32, (rows, cols), 0) % 8
        c_idx = lax.broadcasted_iota(jnp.int32, (rows, cols), 1) % 8
        kept = jnp.where(r_idx == c_idx, ref[...], 0.0).reshape(rows // 8, 8, cols)
        summed = jnp.sum(kept, axis=1)
        offset = (slot * 2 + layer) * C
        pick_r = lax.broadcasted_iota(jnp.int32, (cols, LANES), 0) // 8 + offset
        pick_c = lax.broadcasted_iota(jnp.int32, (cols, LANES), 1)
        pick = jnp.where(pick_r == pick_c, 1.0 / N, 0.0).astype(F32)
        placed = jnp.dot(summed, pick, precision=lax.Precision.HIGHEST, preferred_element_type=F32)
        if rows // 8 < F:
            placed = jnp.concatenate([placed, jnp.zeros((F - rows // 8, LANES), F32)], axis=0)
        total = total + placed
    grads_ref[...] = total


def finish_body(recv_ref, base_ref, ewz_ref, out_ref, grads_ref, left_ref):
    wire_to_rows(recv_ref, left_ref)
    for c2 in range(2):
        r = dot(left_ref[...], ewz_ref[c2]).reshape(CP, ROWS, N)
        out_ref[:, c2] = (base_ref[:, c2].astype(F32) + r).astype(BF)
    grads_ref[...] = jnp.sum(recv_ref[:, WIRE : WIRE + F, :].astype(F32), axis=0)


def to_spectrum(recv_ref, col_ref):
    total = jnp.zeros((WIRE, 4 * M), F32)
    for j in range(SLABS):
        total = total + dot(recv_ref[j], col_ref[j])
    return total


def from_spectrum(values, col_ref, send_ref, scale):
    for j in range(SLABS):
        r = dot_nt(values, col_ref[j])
        if scale != 1.0:
            r = r * scale
        send_ref[j, 0:WIRE, :] = r.astype(BF)


def spectrum_in(ref, value):
    value = value.astype(F32)
    ref[0] = value[:, :LANES]
    ref[1] = value[:, LANES:]


def spectrum_of(ref):
    return jnp.concatenate([ref[0], ref[1]], axis=1).astype(BF)


def interleaved(xa_ref, xb_ref, value):
    value = value.astype(F32)
    re = value[:, :LANES].reshape(C, KB, LANES)
    im = value[:, LANES:].reshape(C, KB, LANES)
    for c in range(C):
        xa_ref[pl.ds(2 * c, KB, stride=2 * C), :] = re[c]
        xa_ref[pl.ds(2 * c + 1, KB, stride=2 * C), :] = -im[c]
        xb_ref[pl.ds(2 * c, KB, stride=2 * C), :] = im[c]
        xb_ref[pl.ds(2 * c + 1, KB, stride=2 * C), :] = re[c]


def mix(spec_ref, xa_ref, xb_ref, y_ref):
    def one(k, carry):
        at = pl.multiple_of(k * 2 * C, 8)
        xa = xa_ref[pl.ds(at, 2 * C), :]
        xb = xb_ref[pl.ds(at, 2 * C), :]
        for o in range(0, C, 2):
            w = spec_ref[k, o * 2 * C : (o + 2) * 2 * C, :].astype(F32)
            for s in range(2):
                r = w[s * 2 * C : (s + 1) * 2 * C]
                row = pl.ds((o + s) * KB + k, 1)
                y_ref[0, row, :] = jnp.sum(r * xa, axis=0, keepdims=True)
                y_ref[1, row, :] = jnp.sum(r * xb, axis=0, keepdims=True)
        return carry

    lax.fori_loop(0, KB, one, 0)


def spectrum_body(recv_ref, col_ref, x_ref):
    x_ref[...] = (to_spectrum(recv_ref, col_ref) * (1.0 / N)).astype(BF)


def mix_body(x_ref, spec_ref, col_ref, *rest):
    send_ref, xa_ref, xb_ref, ys_ref = rest[-4:]
    interleaved(xa_ref, xb_ref, x_ref[...])
    mix(spec_ref, xa_ref, xb_ref, ys_ref)
    from_spectrum(spectrum_of(ys_ref), col_ref, send_ref, 1.0)


def modes_body(recv_ref, spec_ref, col_ref, *rest):
    x_ref, send_ref, xa_ref, xb_ref, ys_ref = rest[-5:]
    x = (to_spectrum(recv_ref, col_ref) * (1.0 / N)).astype(BF)
    x_ref[...] = x
    interleaved(xa_ref, xb_ref, x)
    mix(spec_ref, xa_ref, xb_ref, ys_ref)
    from_spectrum(spectrum_of(ys_ref), col_ref, send_ref, 1.0)


def modes_back_body(tail, *refs):
    refs = list(refs)
    recv_ref, spec_ref, col_ref = refs[:3]
    refs = refs[3:]
    if tail:
        grads_ref = refs.pop(0)
    send_ref, gy_ref, ga_ref, gb_ref, ys_ref, gx_ref = refs
    gy = to_spectrum(recv_ref, col_ref).astype(BF)
    gy_ref[...] = gy
    spectrum_in(ys_ref, gy)

    def one(k, carry):
        acc_a = jnp.zeros((2 * C, LANES), F32)
        acc_b = jnp.zeros((2 * C, LANES), F32)
        for o in range(0, C, 2):
            w = spec_ref[k, o * 2 * C : (o + 2) * 2 * C, :].astype(F32)
            for s in range(2):
                r = w[s * 2 * C : (s + 1) * 2 * C]
                row = pl.ds((o + s) * KB + k, 1)
                acc_a = acc_a + r * ys_ref[0, row, :]
                acc_b = acc_b + r * ys_ref[1, row, :]
        at = pl.multiple_of(k * 2 * C, 8)
        ga_ref[pl.ds(at, 2 * C), :] = acc_a
        gb_ref[pl.ds(at, 2 * C), :] = acc_b
        return carry

    lax.fori_loop(0, KB, one, 0)
    for c in range(C):
        re = pl.ds(2 * c, KB, stride=2 * C)
        im = pl.ds(2 * c + 1, KB, stride=2 * C)
        gx_ref[0, c * KB : (c + 1) * KB, :] = ga_ref[re, :] + gb_ref[im, :]
        gx_ref[1, c * KB : (c + 1) * KB, :] = gb_ref[re, :] - ga_ref[im, :]
    from_spectrum(spectrum_of(gx_ref), col_ref, send_ref, 1.0 / N)
    if tail:
        g = grads_ref[...].astype(BF)
        for j in range(SLABS):
            send_ref[j, WIRE : WIRE + F, :] = g


def spec_grad_body(gy_ref, x_ref, *rest):
    out_ref, ys_ref, xa_ref, xb_ref = rest[-4:]
    k = pl.program_id(0)

    @pl.when(k == 0)
    def _():
        spectrum_in(ys_ref, gy_ref[...])
        interleaved(xa_ref, xb_ref, x_ref[...])

    at = pl.multiple_of(k * 2 * C, 8)
    xa = xa_ref[pl.ds(at, 2 * C), :]
    xb = xb_ref[pl.ds(at, 2 * C), :]
    for o in range(C):
        row = pl.ds(o * KB + k, 1)
        out_ref[o * 2 * C : (o + 1) * 2 * C, :] = ys_ref[0, row, :] * xa + ys_ref[1, row, :] * xb


def prep_body(skip_ref, up_ref, down_ref, ws_ref, wst_ref, w1_ref, w1t_ref, w2_ref, w2t_ref):
    def spread(rows):
        r = lax.broadcasted_iota(jnp.int32, (8 * rows, rows), 0) // 8
        c = lax.broadcasted_iota(jnp.int32, (8 * rows, rows), 1)
        return jnp.where(r == c, 1.0, 0.0).astype(BF)

    wide = {n: spread(n) for n in (C, F)}

    def same(rows, cols):
        r = lax.broadcasted_iota(jnp.int32, (8 * rows, 8 * cols), 0) % 8
        c = lax.broadcasted_iota(jnp.int32, (8 * rows, 8 * cols), 1) % 8
        return r == c

    masks = {(a, b): same(a, b) for a, b in ((C, C), (F, C), (C, F))}

    def expand(weight, a, b, straight_ref, turned_ref, layer):
        rows = dot(wide[a], weight).astype(BF)
        full = dot_nt(rows, wide[b])
        straight_ref[layer] = jnp.where(masks[a, b], full, 0.0).astype(BF)
        cols = dot_nt(wide[b], weight).astype(BF)
        full = dot_nt(cols, wide[a])
        turned_ref[layer] = jnp.where(masks[b, a], full, 0.0).astype(BF)

    for layer in range(LAYERS):
        expand(skip_ref[layer], C, C, ws_ref, wst_ref, layer)
        expand(up_ref[layer], F, C, w1_ref, w1t_ref, layer)
        expand(down_ref[layer], C, F, w2_ref, w2t_ref, layer)


FIELD = (CP, 2, ROWS, N)
LIMIT = pltpu.CompilerParams(vmem_limit_bytes=60 * 1024 * 1024)


def full(shape):
    zeros = (0,) * len(shape)
    return pl.BlockSpec(tuple(shape), lambda *_: zeros)


def part(shape, index):
    return pl.BlockSpec(tuple(shape), lambda *_: tuple(index))


def wire_part(slot, rows=WIRE):
    return part((SLABS, rows, LANES), (0, slot, 0))


def layer_part(shape, layer):
    return part((None,) + tuple(shape), (layer,) + (0,) * len(shape))


def spec_part(layer):
    return part((None, KB, 2 * C * C, LANES), (layer, 0, 0, 0))


def shape_of(shape, dtype):
    return jax.ShapeDtypeStruct(tuple(shape), dtype)


def call(body, name, args, outs, scratch=(), into=None):
    arrays = [a for a, _ in args]
    specs = [s for _, s in args]
    aliases = {}
    if into is not None:
        aliases = {len(arrays): into[0]}
        arrays.append(into[1])
        specs.append(pl.BlockSpec(memory_space=pl.ANY))
        inner, count = body, len(arrays)

        def body(*refs):
            inner(*refs[: count - 1], *refs[count:])

    return pl.pallas_call(
        body,
        out_shape=[o for o, _ in outs],
        grid_spec=pltpu.PrefetchScalarGridSpec(
            num_scalar_prefetch=0,
            grid=(1,),
            in_specs=specs,
            out_specs=[s for _, s in outs],
            scratch_shapes=list(scratch),
        ),
        input_output_aliases=aliases,
        compiler_params=LIMIT,
        name=name,
    )(*arrays)


FIELD_OUT = (shape_of(FIELD, BF), full(FIELD))
LEFT = pltpu.VMEM((CP * ROWS, 4 * M), BF)


def row_dft(field, tabs, slot, slots, into=None):
    out = (shape_of((SLABS, slots * WIRE, LANES), BF), wire_part(slot))
    return call(
        row_dft_body,
        "row_dft",
        [(field, full(FIELD)), (tabs["ew"], full((2 * M, N)))],
        [out],
        into=None if into is None else (0, into),
    )[0]


def forward_rows(wire, slot, field, kron, layer, tabs, keep, last, send_slot=0, slots=1, into=None):
    outs = [FIELD_OUT]
    if not last:
        outs.append((shape_of((SLABS, slots * WIRE, LANES), BF), wire_part(send_slot)))
    if keep:
        outs += [FIELD_OUT, FIELD_OUT]
    return call(
        functools.partial(forward_body, keep, last),
        "forward_rows",
        [
            (wire, wire_part(slot)),
            (field, full(FIELD)),
            (kron["ws"], layer_part((8 * C, 8 * C), layer)),
            (kron["w1"], layer_part((8 * F, 8 * C), layer)),
            (kron["w2"], layer_part((8 * C, 8 * F), layer)),
            (tabs["eiz"], full((2, 4 * M, N))),
            (tabs["ew"], full((2 * M, N))),
        ],
        outs,
        scratch=[LEFT, pltpu.VMEM(FIELD, F32)],
        into=None if into is None else (1, into),
    )


def back_rows(first, layer, wire, field, kron, tabs, top=None, base=None, grads=None, y=None, slope=None):
    args = [
        (wire, wire_part(0)),
        (tabs["eiz" if first else "ewz"], full((2, 4 * M, N))),
        (field, full(FIELD)),
        (kron["wst"], layer_part((8 * C, 8 * C), layer)),
        (kron["w1"], layer_part((8 * F, 8 * C), layer)),
        (kron["w1t"], layer_part((8 * C, 8 * F), layer)),
        (kron["w2t"], layer_part((8 * F, 8 * C), layer)),
        (tabs["ei"], full((2 * M, N))),
    ]
    if first:
        args += [(top, full(FIELD)), (kron["ws"], layer_part((8 * C, 8 * C), layer))]
    else:
        args += [(base, full(FIELD)), (grads, full((F, LANES))), (y, full(FIELD)), (slope, full(FIELD))]
    scratch = [
        pltpu.VMEM(FIELD, BF),
        pltpu.VMEM((8 * F, 8 * C), F32),
        pltpu.VMEM((8 * F, 8 * C), F32),
        pltpu.VMEM((8 * C, 8 * C), F32),
        LEFT,
        pltpu.VMEM(FIELD, F32 if first else BF),
    ]
    return call(
        functools.partial(back_body, first, layer),
        "back_rows",
        args,
        [
            FIELD_OUT,
            (shape_of((SLABS, WIRE, LANES), BF), wire_part(0)),
            (shape_of((F, LANES), F32), full((F, LANES))),
        ],
        scratch=scratch,
    )


SPECTRUM = (WIRE, 4 * M)
SPECTRUM_OUT = (shape_of(SPECTRUM, BF), full(SPECTRUM))
HALF = pltpu.VMEM((2, WIRE, LANES), F32)
MIXED = pltpu.VMEM((2 * WIRE, LANES), F32)
COL = (SLABS, 2 * ROWS, 4 * M)


def spectrum(wire, slot, tabs):
    return call(
        spectrum_body, "spectrum", [(wire, wire_part(slot)), (tabs["col"], full(COL))], [SPECTRUM_OUT]
    )[0]


def mix_out(x, spec, layer, tabs, slot, slots, into=None):
    return call(
        mix_body,
        "mix_out",
        [(x, full(SPECTRUM)), (spec, spec_part(layer)), (tabs["col"], full(COL))],
        [(shape_of((SLABS, slots * WIRE, LANES), BF), wire_part(slot))],
        scratch=[MIXED, MIXED, HALF],
        into=None if into is None else (0, into),
    )[0]


def modes(wire, slot, spec, layer, tabs, send_slot, slots, into=None):
    return call(
        modes_body,
        "modes",
        [(wire, wire_part(slot)), (spec, spec_part(layer)), (tabs["col"], full(COL))],
        [SPECTRUM_OUT, (shape_of((SLABS, slots * WIRE, LANES), BF), wire_part(send_slot))],
        scratch=[MIXED, MIXED, HALF],
        into=None if into is None else (1, into),
    )


def modes_back(wire, spec, layer, tabs, grads=None, slots=1):
    tail = grads is not None
    rows = WIRE + (F if tail else 0)
    args = [(wire, wire_part(0)), (spec, spec_part(layer)), (tabs["col"], full(COL))]
    if tail:
        args.append((grads, full((F, LANES))))
    return call(
        functools.partial(modes_back_body, tail),
        "modes_back",
        args,
        [(shape_of((SLABS, slots * rows, LANES), BF), wire_part(0, rows)), SPECTRUM_OUT],
        scratch=[MIXED, MIXED, HALF, HALF],
    )


def spec_grad(gy, x, layer, into=None):
    args, specs, aliases = [gy, x], [full(SPECTRUM), full(SPECTRUM)], {}
    body = spec_grad_body
    if into is not None:
        args.append(into)
        specs.append(pl.BlockSpec(memory_space=pl.ANY))
        aliases = {2: 0}
    return pl.pallas_call(
        body,
        out_shape=shape_of((LAYERS, KB, 2 * C * C, LANES), F32),
        grid_spec=pltpu.PrefetchScalarGridSpec(
            num_scalar_prefetch=0,
            grid=(KB,),
            in_specs=specs,
            out_specs=pl.BlockSpec(
                (None, None, 2 * C * C, LANES), lambda k: (layer, k, 0, 0)
            ),
            scratch_shapes=[HALF, MIXED, MIXED],
        ),
        input_output_aliases=aliases,
        compiler_params=LIMIT,
        name="spec_grad",
    )(*args)


def finish(wire, base, tabs):
    rows = WIRE + F
    return call(
        finish_body,
        "finish",
        [(wire, wire_part(0, rows)), (base, full(FIELD)), (tabs["ewz"], full((2, 4 * M, N)))],
        [FIELD_OUT, (shape_of((F, LANES), F32), full((F, LANES)))],
        scratch=[LEFT],
    )


def prep(skip_w, up_w, down_w):
    names = ["ws", "wst", "w1", "w1t", "w2", "w2t"]
    sizes = [(C, C), (C, C), (F, C), (C, F), (C, F), (F, C)]
    outs = [(LAYERS, 8 * a, 8 * b) for a, b in sizes]
    res = call(
        prep_body,
        "prep",
        [(w, part((None,) + w.shape[1:], (0,) * w.ndim)) for w in (skip_w, up_w, down_w)],
        [(shape_of(o, BF), full(o)) for o in outs],
    )
    return dict(zip(names, res))


def exchange(wire):
    return lax.all_to_all(wire, "slab", split_axis=0, concat_axis=0, tiled=True)


def shifted(block, distance):
    count = lax.axis_size("section")
    return lax.ppermute(block, "section", [(i, (i + distance) % count) for i in range(count)])


def shards(emitted, returned, stash, skip_w, up_w, down_w, spec_w):
    tabs = {name: jnp.asarray(value) for name, value in np_tables().items()}
    half = lax.axis_size("section") // 2
    emitted = emitted.reshape(FIELD)
    returned = returned.reshape(FIELD)
    stash = stash.reshape(FIELD)
    spec_w = spec_w[0].transpose(0, 1, 3, 4, 2, 5).reshape(LAYERS, KB, 2 * C * C, LANES)
    kron = prep(skip_w, up_w, down_w)
    kept_a = shifted(stash[:EARLY], half)

    wire = row_dft(stash, tabs, 0, 2)
    wire = row_dft(emitted, tabs, 1, 2, into=wire)
    wire = exchange(wire)
    x_0 = shifted(spectrum(wire, 0, tabs), half)
    ahead_x = shifted(spectrum(wire, 1, tabs), 1)
    stash_b, emitted, x_0, ahead_x = lax.optimization_barrier((stash[EARLY:], emitted, x_0, ahead_x))
    kept_b = shifted(stash_b, half)
    ahead = shifted(emitted, 1)
    kept = jnp.concatenate([kept_a, kept_b], axis=0)

    wire = mix_out(x_0, spec_w, 0, tabs, 0, 2)
    wire = mix_out(ahead_x, spec_w, 0, tabs, 1, 2, into=wire)
    first_wire = exchange(wire)
    kept_1, out, y_0, slope_0 = forward_rows(first_wire, 0, kept, kron, 0, tabs, True, False)
    returned, out = lax.optimization_barrier((returned, out))
    wire = exchange(out)
    top = shifted(returned, -1)
    x_1, out = modes(wire, 0, spec_w, 1, tabs, 0, 2)
    ahead_1, out = forward_rows(first_wire, 1, ahead, kron, 0, tabs, False, False, 1, 2, into=out)
    second_wire = exchange(out)

    base, out, grads = back_rows(True, 1, second_wire, kept_1, kron, tabs, top=top)
    wire = exchange(out)
    out, gy_1 = modes_back(wire, spec_w, 1, tabs, slots=2)
    _, out = modes(second_wire, 1, spec_w, 1, tabs, 1, 2, into=out)
    third_wire = exchange(out)
    grad_spec = spec_grad(gy_1, x_1, 1)
    base, out, grads = back_rows(
        False, 0, third_wire, kept, kron, tabs, base=base, grads=grads, y=y_0, slope=slope_0
    )
    wire = exchange(out)
    (sent,) = forward_rows(third_wire, 1, ahead_1, kron, 1, tabs, False, True)
    out, gy_0 = modes_back(wire, spec_w, 0, tabs, grads)
    wire = exchange(out)
    grad_spec = spec_grad(gy_0, x_0, 0, into=grad_spec)
    back_grad, packed = finish(wire, base, tabs)

    def slot(number):
        return jnp.stack([packed[:, (number * 2 + l) * C : (number * 2 + l + 1) * C] for l in range(LAYERS)])

    grad_down = jnp.swapaxes(slot(0), 1, 2)
    grad_up = slot(1)
    grad_skip = slot(2)[:, :C]
    field = (1, C, ROWS, N)
    return (
        sent.reshape(field),
        back_grad.reshape(field),
        grad_skip[None],
        grad_up[None],
        grad_down[None],
        grad_spec.reshape(LAYERS, KB, C, C, 2, LANES).transpose(0, 1, 4, 2, 3, 5)[None],
    )


def solution(mesh):
    field = P("section", None, "slab", None)
    weight = P("section", None, None, None)
    spec = P("section", None, "slab", None, None, None, None)
    return jax.shard_map(
        shards,
        mesh=mesh,
        in_specs=(field, field, field, weight, weight, weight, spec),
        out_specs=(field, field, weight, weight, weight, spec),
        check_vma=False,
    )
```

profile of v0, /device:TPU:2, one launch (start us, length us, event | category | flops | bytes accessed | tf_op | source)
XLA Modules:
  0.0 238.0 jit_solution(18409884324163274152)
XLA Ops:
  6.0 6.3 %all-to-all-start = ((bf16[8,320,128]{2,1,0:T(8,128)(2,1)}), bf16[8,320,128]{2,1,0:T(8,128)(2,1)S(1)}, u32[]{:S(2)}, u32[]{:S(2)}) async-start(bf16[8,320,128]{2,1,0:T(8,128)(2,1)} %row_dft.3), calls=%async_computation | async-start | bytes 1310720 | tf_op jit(solution)/shard_map/all_to_all | solution.py:644
  13.5 3.6 %collective-permute-start.3 = (bf16[5,2,64,512]{3,2,1,0:T(8,128)(2,1)}, bf16[5,2,64,512]{3,2,1,0:T(8,128)(2,1)}, u32[]{:S(2)}, u32[]{:S(2)}) collective-permute-start(bf16[5,2,64,512]{3,2,1,0:T(8,128)(2,1)} %bitcast.9), channel_id=1, source_target_pairs={{0,64},{8,72},{16,80},{24,88},{32,96},{40,104},{48,112},{56,120},{... | collective-permute-start | bytes 1966088 | tf_op jit(solution)/shard_map/ppermute | solution.py:649
  17.1 5.2 %all-to-all-done.recv_ref = bf16[8,320,128]{2,1,0:T(8,128)(2,1)S(1)} async-done(((bf16[8,320,128]{2,1,0:T(8,128)(2,1)}), bf16[8,320,128]{2,1,0:T(8,128)(2,1)S(1)}, u32[]{:S(2)}, u32[]{:S(2)}) %all-to-all-start) | async-done | bytes 655392 | tf_op jit(solution)/shard_map/all_to_all | solution.py:644
  25.3 3.8 %collective-permute-start = (bf16[160,256]{1,0:T(8,128)(2,1)}, bf16[160,256]{1,0:T(8,128)(2,1)S(1)}, u32[]{:S(2)}, u32[]{:S(2)}) collective-permute-start(bf16[160,256]{1,0:T(8,128)(2,1)} %spectrum.2), channel_id=1, source_target_pairs={{0,64},{8,72},{16,80},{24,88},{32,96},{40,104},{48,112},{56,120},{... | collective-permute-start | bytes 245768 | tf_op jit(solution)/shard_map/ppermute | solution.py:649
  31.1 8.5 %collective-permute-done.x_ref = bf16[160,256]{1,0:T(8,128)(2,1)S(1)} collective-permute-done((bf16[160,256]{1,0:T(8,128)(2,1)}, bf16[160,256]{1,0:T(8,128)(2,1)S(1)}, u32[]{:S(2)}, u32[]{:S(2)}) %collective-permute-start) | collective-permute-done | bytes 81952 | tf_op jit(solution)/shard_map/ppermute | solution.py:649
  47.2 5.5 %all-to-all-start.1 = ((bf16[8,320,128]{2,1,0:T(8,128)(2,1)}), bf16[8,320,128]{2,1,0:T(8,128)(2,1)S(1)}, u32[]{:S(2)}, u32[]{:S(2)}) async-start(bf16[8,320,128]{2,1,0:T(8,128)(2,1)} %mix_out.3), calls=%async_computation.1 | async-start | bytes 1310720 | tf_op jit(solution)/shard_map/all_to_all | solution.py:644
  59.3 18.9 %collective-permute-done.4 = bf16[5,2,64,512]{3,2,1,0:T(8,128)(2,1)} collective-permute-done((bf16[5,2,64,512]{3,2,1,0:T(8,128)(2,1)}, bf16[5,2,64,512]{3,2,1,0:T(8,128)(2,1)}, u32[]{:S(2)}, u32[]{:S(2)}) %collective-permute-start.4) | collective-permute-done | bytes 655392 | tf_op jit(solution)/shard_map/ppermute | solution.py:649
  80.6 8.7 %forward_rows.3 = (bf16[10,2,64,512]{3,2,1,0:T(8,128)(2,1)}, bf16[8,160,128]{2,1,0:T(8,128)(2,1)}, bf16[10,2,64,512]{3,2,1,0:T(8,128)(2,1)}, bf16[10,2,64,512]{3,2,1,0:T(8,128)(2,1)}) custom-call(bf16[8,320,128]{2,1,0:T(8,128)(2,1)} %copy-done.2, bf16[10,2,64,512]{3,2,1,0:T(8,128)(2,1)} %copy-done, bf16[2,160,160]{2,1,0:T(8,128)(2,1)} %get-tuple-element.42.refs_2_.refs_9_, ...), custom_call_target="tpu_custom_call" | custom-call | tf_op jit(solution)/shard_map/forward_rows/pallas_call | solution.py:453
  89.3 12.6 %all_to_all.40.recv_ref = bf16[8,160,128]{2,1,0:T(8,128)(2,1)} all-to-all(bf16[8,160,128]{2,1,0:T(8,128)(2,1)} %get-tuple-element.47), channel_id=1, replica_groups=mesh['section'=16,'slab'=8] {'slab'}, dimensions={0} | all-to-all | bytes 655360 | tf_op jit(solution)/shard_map/all_to_all | solution.py:644
  101.9 4.2 %modes.2 = (bf16[160,256]{1,0:T(8,128)(2,1)}, bf16[8,320,128]{2,1,0:T(8,128)(2,1)}) custom-call(bf16[8,160,128]{2,1,0:T(8,128)(2,1)} %all_to_all.40.recv_ref, bf16[2,8,800,128]{3,2,1,0:T(8,128)(2,1)} %bitcast.39, bf16[8,128,256]{2,1,0:T(8,128)(2,1)} %constant.14.clone.col_ref.refs_2_), custom_call_target="tpu_custom_call" | custom-call | tf_op jit(solution)/shard_map/modes/pallas_call | solution.py:453
  106.1 8.0 %forward_rows.4 = (bf16[10,2,64,512]{3,2,1,0:T(8,128)(2,1)}, bf16[8,320,128]{2,1,0:T(8,128)(2,1)}) custom-call(bf16[8,320,128]{2,1,0:T(8,128)(2,1)} %copy-done.2, bf16[10,2,64,512]{3,2,1,0:T(8,128)(2,1)} %collective-permute-done.2.refs_1_, bf16[2,160,160]{2,1,0:T(8,128)(2,1)} %get-tuple-element.42.refs_2_.refs_9_, ...), custom_call_target="tpu_custom_call", output_to_operand_aliasing={{1}: (7, {})} | custom-call | tf_op jit(solution)/shard_map/forward_rows/pallas_call | solution.py:453
  114.0 15.0 %all_to_all.41.refs_0_ = bf16[8,320,128]{2,1,0:T(8,128)(2,1)} all-to-all(bf16[8,320,128]{2,1,0:T(8,128)(2,1)} %get-tuple-element.49), channel_id=1, replica_groups=mesh['section'=16,'slab'=8] {'slab'}, dimensions={0} | all-to-all | bytes 1310720 | tf_op jit(solution)/shard_map/all_to_all | solution.py:644
  130.1 15.3 %back_rows.2 = (bf16[10,2,64,512]{3,2,1,0:T(8,128)(2,1)}, bf16[8,160,128]{2,1,0:T(8,128)(2,1)}, f32[80,128]{1,0:T(8,128)}) custom-call(bf16[8,320,128]{2,1,0:T(8,128)(2,1)} %all_to_all.41.refs_0_, bf16[2,256,512]{2,1,0:T(8,128)(2,1)} %constant.13.clone.refs_5_.refs_1_, bf16[10,2,64,512]{3,2,1,0:T(8,128)(2,1)} %get-tuple-element.50.refs_2_, ...), custom_call_target="tpu_custom_call" | custom-call | tf_op jit(solution)/shard_map/back_rows/pallas_call | solution.py:453
  145.4 11.8 %all_to_all.42.refs_0_ = bf16[8,160,128]{2,1,0:T(8,128)(2,1)} all-to-all(bf16[8,160,128]{2,1,0:T(8,128)(2,1)} %get-tuple-element.55), channel_id=1, replica_groups=mesh['section'=16,'slab'=8] {'slab'}, dimensions={0} | all-to-all | bytes 655360 | tf_op jit(solution)/shard_map/all_to_all | solution.py:644
  157.2 4.1 %modes_back.2 = (bf16[8,320,128]{2,1,0:T(8,128)(2,1)}, bf16[160,256]{1,0:T(8,128)(2,1)}) custom-call(bf16[8,160,128]{2,1,0:T(8,128)(2,1)} %all_to_all.42.refs_0_, bf16[2,8,800,128]{3,2,1,0:T(8,128)(2,1)} %bitcast.40, bf16[8,128,256]{2,1,0:T(8,128)(2,1)} %constant.14.clone.col_ref.refs_2_), custom_call_target="tpu_custom_call" | custom-call | tf_op jit(solution)/shard_map/modes_back/pallas_call | solution.py:453
  161.3 4.1 %modes.3 = (bf16[160,256]{1,0:T(8,128)(2,1)}, bf16[8,320,128]{2,1,0:T(8,128)(2,1)}) custom-call(bf16[8,320,128]{2,1,0:T(8,128)(2,1)} %all_to_all.41.refs_0_, bf16[2,8,800,128]{3,2,1,0:T(8,128)(2,1)} %bitcast.41, bf16[8,128,256]{2,1,0:T(8,128)(2,1)} %constant.14.clone.col_ref.refs_2_, ...), custom_call_target="tpu_custom_call", output_to_operand_aliasing={{1}: (3, {})} | custom-call | tf_op jit(solution)/shard_map/modes/pallas_call | solution.py:453
  165.4 13.3 %all_to_all.43.refs_0_ = bf16[8,320,128]{2,1,0:T(8,128)(2,1)} all-to-all(bf16[8,320,128]{2,1,0:T(8,128)(2,1)} %get-tuple-element.57), channel_id=1, replica_groups=mesh['section'=16,'slab'=8] {'slab'}, dimensions={0} | all-to-all | bytes 1310720 | tf_op jit(solution)/shard_map/all_to_all | solution.py:644
  178.7 15.1 %back_rows.3 = (bf16[10,2,64,512]{3,2,1,0:T(8,128)(2,1)}, bf16[8,160,128]{2,1,0:T(8,128)(2,1)}, f32[80,128]{1,0:T(8,128)}) custom-call(bf16[8,320,128]{2,1,0:T(8,128)(2,1)} %all_to_all.43.refs_0_, bf16[2,256,512]{2,1,0:T(8,128)(2,1)} %constant.12.clone.refs_1_.ewz_ref, bf16[10,2,64,512]{3,2,1,0:T(8,128)(2,1)} %copy-done, ...), custom_call_target="tpu_custom_call" | custom-call | tf_op jit(solution)/shard_map/back_rows/pallas_call | solution.py:453
  193.8 11.8 %all_to_all.44.refs_0_ = bf16[8,160,128]{2,1,0:T(8,128)(2,1)} all-to-all(bf16[8,160,128]{2,1,0:T(8,128)(2,1)} %get-tuple-element.63), channel_id=1, replica_groups=mesh['section'=16,'slab'=8] {'slab'}, dimensions={0} | all-to-all | bytes 655360 | tf_op jit(solution)/shard_map/all_to_all | solution.py:644
  205.6 4.1 %modes_back.3 = (bf16[8,240,128]{2,1,0:T(8,128)(2,1)}, bf16[160,256]{1,0:T(8,128)(2,1)}) custom-call(bf16[8,160,128]{2,1,0:T(8,128)(2,1)} %all_to_all.44.refs_0_, bf16[2,8,800,128]{3,2,1,0:T(8,128)(2,1)} %bitcast.42, bf16[8,128,256]{2,1,0:T(8,128)(2,1)} %constant.14.clone.col_ref.refs_2_, f32[80,128]{1,0:T(8,128)} %get-tuple-element.64.refs_3_), custom_call_target="tpu_custom_call" | custom-call | tf_op jit(solution)/shard_map/modes_back/pallas_call | solution.py:453
  209.7 4.8 %all-to-all-start.7 = ((bf16[8,240,128]{2,1,0:T(8,128)(2,1)}), bf16[8,240,128]{2,1,0:T(8,128)(2,1)S(1)}, u32[]{:S(2)}, u32[]{:S(2)}) async-start(bf16[8,240,128]{2,1,0:T(8,128)(2,1)} %get-tuple-element.65), calls=%async_computation.7 | async-start | bytes 983040 | tf_op jit(solution)/shard_map/all_to_all | solution.py:644
  214.6 4.3 %spec_grad.2.rest_0_ = f32[2,8,800,128]{3,2,1,0:T(8,128)} custom-call(bf16[160,256]{1,0:T(8,128)(2,1)} %get-tuple-element.70.gy_ref, bf16[160,256]{1,0:T(8,128)(2,1)} %get-tuple-element.71.x_ref), custom_call_target="tpu_custom_call" | custom-call | tf_op jit(solution)/shard_map/spec_grad/pallas_call | solution.py:601
  218.9 7.7 %forward_rows.5 = bf16[10,2,64,512]{3,2,1,0:T(8,128)(2,1)} custom-call(bf16[8,320,128]{2,1,0:T(8,128)(2,1)} %all_to_all.43.refs_0_, bf16[10,2,64,512]{3,2,1,0:T(8,128)(2,1)} %get-tuple-element.58.refs_1_, bf16[2,160,160]{2,1,0:T(8,128)(2,1)} %get-tuple-element.42.refs_2_.refs_9_, bf16[2,640,160]{2,1,0:T(8,128)(2,1)} %get-tuple-element.43.refs_3_.refs_4_, ...), custom_call_target="tpu_custom_call" | custom-call | tf_op jit(solution)/shard_map/forward_rows/pallas_call | solution.py:453
  226.5 4.3 %spec_grad.3 = f32[2,8,800,128]{3,2,1,0:T(8,128)} custom-call(bf16[160,256]{1,0:T(8,128)(2,1)} %get-tuple-element.69.gy_ref, bf16[160,256]{1,0:T(8,128)(2,1)} %copy-done.7, f32[2,8,800,128]{3,2,1,0:T(8,128)} %spec_grad.2.rest_0_), custom_call_target="tpu_custom_call", output_to_operand_aliasing={{}: (2, {})} | custom-call | tf_op jit(solution)/shard_map/spec_grad/pallas_call | solution.py:601
  (58 shorter events, 36.3 us)
Async XLA Ops:
  6.0 6.3 %copy-start.3 = (bf16[1,20,64,512]{3,2,1,0:T(8,128)(2,1)S(1)}, bf16[1,20,64,512]{3,2,1,0:T(8,128)(2,1)}, u32[]{:S(2)}) copy-start(bf16[1,20,64,512]{3,2,1,0:T(8,128)(2,1)} %param.14) | copy-start | bytes 3932164
  6.0 16.3 %all-to-all-start = ((bf16[8,320,128]{2,1,0:T(8,128)(2,1)}), bf16[8,320,128]{2,1,0:T(8,128)(2,1)S(1)}, u32[]{:S(2)}, u32[]{:S(2)}) async-start(bf16[8,320,128]{2,1,0:T(8,128)(2,1)} %row_dft.3), calls=%async_computation | async-start | bytes 1310720 | tf_op jit(solution)/shard_map/all_to_all | solution.py:644
  13.5 44.6 %collective-permute-start.3 = (bf16[5,2,64,512]{3,2,1,0:T(8,128)(2,1)}, bf16[5,2,64,512]{3,2,1,0:T(8,128)(2,1)}, u32[]{:S(2)}, u32[]{:S(2)}) collective-permute-start(bf16[5,2,64,512]{3,2,1,0:T(8,128)(2,1)} %bitcast.9), channel_id=1, source_target_pairs={{0,64},{8,72},{16,80},{24,88},{32,96},{40,104},{48,112},{56,120},{... | collective-permute-start | bytes 1966088 | tf_op jit(solution)/shard_map/ppermute | solution.py:649
  22.3 0.8 copy-start.1
  25.3 14.4 %collective-permute-start = (bf16[160,256]{1,0:T(8,128)(2,1)}, bf16[160,256]{1,0:T(8,128)(2,1)S(1)}, u32[]{:S(2)}, u32[]{:S(2)}) collective-permute-start(bf16[160,256]{1,0:T(8,128)(2,1)} %spectrum.2), channel_id=1, source_target_pairs={{0,64},{8,72},{16,80},{24,88},{32,96},{40,104},{48,112},{56,120},{... | collective-permute-start | bytes 245768 | tf_op jit(solution)/shard_map/ppermute | solution.py:649
  31.1 8.5 %collective-permute-start.1 = (bf16[160,256]{1,0:T(8,128)(2,1)}, bf16[160,256]{1,0:T(8,128)(2,1)S(1)}, u32[]{:S(2)}, u32[]{:S(2)}) collective-permute-start(bf16[160,256]{1,0:T(8,128)(2,1)} %spectrum.3), channel_id=1, source_target_pairs={{0,8},{8,16},{16,24},{24,32},{32,40},{40,48},{48,56},{56,64},{64,7... | collective-permute-start | bytes 245768 | tf_op jit(solution)/shard_map/ppermute | solution.py:649
  39.6 0.6 copy-start.7
  39.6 4.1 %copy-start.8 = (bf16[160,256]{1,0:T(8,128)(2,1)}, bf16[160,256]{1,0:T(8,128)(2,1)S(1)}, u32[]{:S(2)}) copy-start(bf16[160,256]{1,0:T(8,128)(2,1)S(1)} %collective-permute-done.1.refs_0_) | copy-start | bytes 245764
  39.7 38.5 %collective-permute-start.4 = (bf16[5,2,64,512]{3,2,1,0:T(8,128)(2,1)}, bf16[5,2,64,512]{3,2,1,0:T(8,128)(2,1)}, u32[]{:S(2)}, u32[]{:S(2)}) collective-permute-start(bf16[5,2,64,512]{3,2,1,0:T(8,128)(2,1)} %bitcast), channel_id=1, source_target_pairs={{0,64},{8,72},{16,80},{24,88},{32,96},{40,104},{48,112},{56,120},{... | collective-permute-start | bytes 1966088 | tf_op jit(solution)/shard_map/ppermute | solution.py:649
  43.7 9.0 %copy-start.9 = (bf16[1,2,20,20]{3,1,2,0:T(2,128)(2,1)S(1)}, bf16[1,2,20,20]{3,1,2,0:T(2,128)(2,1)}, u32[]{:S(2)}) copy-start(bf16[1,2,20,20]{3,1,2,0:T(2,128)(2,1)} %param.15) | copy-start | bytes 4804
  47.2 5.5 %copy-start.5 = (bf16[1,20,64,512]{3,2,1,0:T(8,128)(2,1)S(1)}, bf16[1,20,64,512]{3,2,1,0:T(8,128)(2,1)}, u32[]{:S(2)}) copy-start(bf16[1,20,64,512]{3,2,1,0:T(8,128)(2,1)} %param.12) | copy-start | bytes 3932164
  47.2 6.1 %copy-start.10 = (bf16[1,2,20,80]{3,1,2,0:T(2,128)(2,1)S(1)}, bf16[1,2,20,80]{3,1,2,0:T(2,128)(2,1)}, u32[]{:S(2)}) copy-start(bf16[1,2,20,80]{3,1,2,0:T(2,128)(2,1)} %param.17) | copy-start | bytes 19204
  47.2 6.8 %copy-start.11 = (bf16[1,2,80,20]{2,1,3,0:T(2,128)(2,1)S(1)}, bf16[1,2,80,20]{2,1,3,0:T(2,128)(2,1)}, u32[]{:S(2)}) copy-start(bf16[1,2,80,20]{2,1,3,0:T(2,128)(2,1)} %param.16) | copy-start | bytes 19204
  47.2 32.1 %all-to-all-start.1 = ((bf16[8,320,128]{2,1,0:T(8,128)(2,1)}), bf16[8,320,128]{2,1,0:T(8,128)(2,1)S(1)}, u32[]{:S(2)}, u32[]{:S(2)}) async-start(bf16[8,320,128]{2,1,0:T(8,128)(2,1)} %mix_out.3), calls=%async_computation.1 | async-start | bytes 1310720 | tf_op jit(solution)/shard_map/all_to_all | solution.py:644
  52.8 53.3 %collective-permute-start.2 = (bf16[10,2,64,512]{3,2,1,0:T(8,128)(2,1)S(1)}, bf16[10,2,64,512]{3,2,1,0:T(8,128)(2,1)}, u32[]{:S(2)}, u32[]{:S(2)}) collective-permute-start(bf16[10,2,64,512]{3,2,1,0:T(8,128)(2,1)S(1)} %bitcast.47), channel_id=1, source_target_pairs={{0,8},{8,16},{16,24},{24,32},{32,40},{40,48},{48,56},{56,64},{64,7... | collective-permute-start | bytes 3932168 | tf_op jit(solution)/shard_map/ppermute | solution.py:649
  79.3 1.1 copy-start
  79.4 1.3 copy-start.2
  89.3 39.7 %collective-permute-start.5 = (bf16[10,2,64,512]{3,2,1,0:T(8,128)(2,1)}, bf16[10,2,64,512]{3,2,1,0:T(8,128)(2,1)S(1)}, u32[]{:S(2)}, u32[]{:S(2)}) collective-permute-start(bf16[10,2,64,512]{3,2,1,0:T(8,128)(2,1)} %bitcast.48), channel_id=1, source_target_pairs={{0,120},{8,0},{16,8},{24,16},{32,24},{40,32},{48,40},{56,48},{64,5... | collective-permute-start | bytes 3932168 | tf_op jit(solution)/shard_map/ppermute | solution.py:649
  129.0 1.1 copy-start.6
  209.7 21.1 %all-to-all-start.7 = ((bf16[8,240,128]{2,1,0:T(8,128)(2,1)}), bf16[8,240,128]{2,1,0:T(8,128)(2,1)S(1)}, u32[]{:S(2)}, u32[]{:S(2)}) async-start(bf16[8,240,128]{2,1,0:T(8,128)(2,1)} %get-tuple-element.65), calls=%async_computation.7 | async-start | bytes 983040 | tf_op jit(solution)/shard_map/all_to_all | solution.py:644
  230.8 0.8 copy-start.4
where the time goes:
time: 240 us; the launch traced here: 238 us
  Pallas kernels  103 us (43%)
  blocking collectives  64.4 us (27%)
  waiting for transfers between devices  32.7 us (14%)
  starting transfers between devices  24.1 us (10%)
  local copies, waits for them, and re-layouts  12.3 us (5%)
    pallas_call x17, Pallas kernels, call(): pl.pallas_call(body, out_shape=[o for o, _ in outs], grid_spec=pltpu.Pref...  94.4 us
    all_to_all x5, blocking collectives, exchange(): return lax.all_to_all(wire, 'slab', split_axis=0, concat_axis=0, tiled=True)  64.4 us
    ppermute x6, waiting for transfers between devices, shifted(): lax.ppermute(block, 'section', [(i, (i + distance) % count) for i in rang...  27.4 us
    all_to_all x3, starting transfers between devices, exchange(): return lax.all_to_all(wire, 'slab', split_axis=0, concat_axis=0, tiled=True)  16.7 us
    pallas_call x2, Pallas kernels, spec_grad(): pl.pallas_call(body, out_shape=shape_of((LAYERS, KB, 2 * C * C, LANES), F...  8.62 us
    unnamed x29, local copies, waits for them, and re-layouts  8.29 us
    ppermute x6, starting transfers between devices, shifted(): lax.ppermute(block, 'section', [(i, (i + distance) % count) for i in rang...  7.41 us
    all_to_all x3, waiting for transfers between devices, exchange(): return lax.all_to_all(wire, 'slab', split_axis=0, concat_axis=0, tiled=True)  5.25 us
  transfers between devices with their start and end apart: 9, of which 3 were waited for; matrix products, arithmetic and copies ran while one was open for 2% of the time, Pallas kernels for 22%

commit v1 on v0

--- a/solution.py
+++ b/solution.py
@@ -18,7 +18,8 @@
 ROWS = N // SLABS
 KB = M // SLABS
 CP = C // 2
-EARLY = CP // 2
+STEP = 4
+CUTS = (CP // 2, CP * 4 // 5)
 WIRE = C * KB
 LANES = 128
 BF = jnp.bfloat16
@@ -125,6 +126,11 @@
     return jnp.concatenate([x[:, :, s * 8 : s * 8 + 8, :].reshape(8 * C, N) for s in range(2)], axis=1)
 
 
+def both(refs, where):
+    blocks = [ref[where] for ref in refs]
+    return blocks[0] if len(blocks) == 1 else jnp.concatenate(blocks, axis=0)
+
+
 def narrow(x):
     parts = [x[:, s * N : (s + 1) * N].reshape(CP, 2, 8, N) for s in range(2)]
     return jnp.concatenate(parts, axis=2).astype(BF)
@@ -142,9 +148,10 @@
     rows_to_wire(field_read(v_ref), table_ref, send_ref)
 
 
-def forward_body(keep, last, *refs):
-    u_ref, v_ref, ws_ref, w1_ref, w2_ref, eiz_ref, ew_ref = refs[:7]
-    outs = list(refs[7:])
+def forward_body(keep, last, parts, *refs):
+    v_refs, refs = refs[:parts], refs[parts:]
+    u_ref, ws_ref, w1_ref, w2_ref, eiz_ref, ew_ref = refs[:6]
+    outs = list(refs[6:])
     left_ref, z_ref = outs[-2:]
     outs = outs[:-2]
     out_ref = outs[0]
@@ -161,7 +168,7 @@
     def step(i, carry):
         h0 = pl.multiple_of(i * 16, 16)
         where = (slice(None), slice(None), pl.ds(h0, 16))
-        v = wide(v_ref[where])
+        v = wide(both(v_refs, where))
         z = wide(z_ref[where]) + dot(ws_ref[...], v.astype(BF))
         if keep:
             y, slope = gate_and_slope(z)
@@ -178,15 +185,15 @@
         rows_to_wire(field_read(out_ref), ew_ref, send_ref)
 
 
-def back_body(first, layer, *refs):
-    refs = list(refs)
-    u_ref, table_ref, v_ref, wst_ref, w1_ref, w1t_ref, w2t_ref, ei_ref = refs[:8]
+def back_body(first, layer, parts, *refs):
+    v_refs, refs = refs[:parts], refs[parts:]
+    u_ref, table_ref, wst_ref, w1_ref, w1t_ref, w2t_ref, ei_ref = refs[:7]
     if first:
-        g_ref, ws_ref = refs[8:10]
-        refs = refs[10:]
+        g_ref, ws_ref = refs[7:9]
+        refs = refs[9:]
     else:
-        base_in_ref, grads_in_ref, y_ref, slope_ref = refs[8:12]
-        refs = refs[12:]
+        base_in_ref, grads_in_ref, y_ref, slope_ref = refs[7:11]
+        refs = refs[11:]
     base_ref, send_ref, grads_ref, gz_ref, gd_ref, gu_ref, gs_ref, left_ref, field_ref = refs
     wire_to_rows(u_ref, left_ref)
     for c2 in range(2):
@@ -205,7 +212,7 @@
         where = (slice(None), slice(None), pl.ds(h0, 16))
         g = wide(g_ref[where])
         gb = g.astype(BF)
-        v = wide(v_ref[where]).astype(BF)
+        v = wide(both(v_refs, where)).astype(BF)
         if first:
             y, out_slope = gate_and_slope(wide(field_ref[where]) + dot(ws_ref[...], v))
             out_slope = out_slope.astype(F32)
@@ -219,7 +226,7 @@
         gz_ref[where] = narrow(gz.astype(F32))
         gd_ref[...] += dot_nt(act.astype(BF), gb)
         gu_ref[...] += dot_nt(gh, y)
-        gs_ref[...] += dot_nt(gz, v)
+        gs_ref[...] += dot_nt(v, gz)
         return carry
 
     lax.fori_loop(0, ROWS // 16, step, 0)
@@ -231,8 +238,8 @@
         c_idx = lax.broadcasted_iota(jnp.int32, (rows, cols), 1) % 8
         kept = jnp.where(r_idx == c_idx, ref[...], 0.0).reshape(rows // 8, 8, cols)
         summed = jnp.sum(kept, axis=1)
-        offset = (slot * 2 + layer) * C
-        pick_r = lax.broadcasted_iota(jnp.int32, (cols, LANES), 0) // 8 + offset
+        offset = slot * 2 * C + layer
+        pick_r = lax.broadcasted_iota(jnp.int32, (cols, LANES), 0) // 8 * 2 + offset
         pick_c = lax.broadcasted_iota(jnp.int32, (cols, LANES), 1)
         pick = jnp.where(pick_r == pick_c, 1.0 / N, 0.0).astype(F32)
         placed = jnp.dot(summed, pick, precision=lax.Precision.HIGHEST, preferred_element_type=F32)
@@ -242,12 +249,15 @@
     grads_ref[...] = total
 
 
-def finish_body(recv_ref, base_ref, ewz_ref, out_ref, grads_ref, left_ref):
+def finish_body(recv_ref, base_ref, ewz_ref, out_ref, down_ref, up_ref, skip_ref, left_ref):
     wire_to_rows(recv_ref, left_ref)
     for c2 in range(2):
         r = dot(left_ref[...], ewz_ref[c2]).reshape(CP, ROWS, N)
         out_ref[:, c2] = (base_ref[:, c2].astype(F32) + r).astype(BF)
-    grads_ref[...] = jnp.sum(recv_ref[:, WIRE : WIRE + F, :].astype(F32), axis=0)
+    grads = jnp.sum(recv_ref[:, WIRE : WIRE + F, :].astype(F32), axis=0).T
+    down_ref[...] = grads[: 2 * C]
+    up_ref[...] = grads[2 * C : 4 * C]
+    skip_ref[...] = grads[4 * C : 6 * C, :C]
 
 
 def to_spectrum(recv_ref, col_ref):
@@ -364,19 +374,19 @@
 
 def spec_grad_body(gy_ref, x_ref, *rest):
     out_ref, ys_ref, xa_ref, xb_ref = rest[-4:]
-    k = pl.program_id(0)
-
-    @pl.when(k == 0)
+    @pl.when(pl.program_id(0) == 0)
     def _():
         spectrum_in(ys_ref, gy_ref[...])
         interleaved(xa_ref, xb_ref, x_ref[...])
 
-    at = pl.multiple_of(k * 2 * C, 8)
-    xa = xa_ref[pl.ds(at, 2 * C), :]
-    xb = xb_ref[pl.ds(at, 2 * C), :]
-    for o in range(C):
-        row = pl.ds(o * KB + k, 1)
-        out_ref[o * 2 * C : (o + 1) * 2 * C, :] = ys_ref[0, row, :] * xa + ys_ref[1, row, :] * xb
+    for m in range(STEP):
+        k = pl.program_id(0) * STEP + m
+        at = pl.multiple_of(k * 2 * C, 8)
+        xa = xa_ref[pl.ds(at, 2 * C), :]
+        xb = xb_ref[pl.ds(at, 2 * C), :]
+        for o in range(C):
+            row = pl.ds(o * KB + k, 1)
+            out_ref[m, o * 2 * C : (o + 1) * 2 * C, :] = ys_ref[0, row, :] * xa + ys_ref[1, row, :] * xb
 
 
 def prep_body(skip_ref, up_ref, down_ref, ws_ref, wst_ref, w1_ref, w1t_ref, w2_ref, w2t_ref):
@@ -488,11 +498,11 @@
     if keep:
         outs += [FIELD_OUT, FIELD_OUT]
     return call(
-        functools.partial(forward_body, keep, last),
+        functools.partial(forward_body, keep, last, len(field)),
         "forward_rows",
-        [
+        [(f, full(f.shape)) for f in field]
+        + [
             (wire, wire_part(slot)),
-            (field, full(FIELD)),
             (kron["ws"], layer_part((8 * C, 8 * C), layer)),
             (kron["w1"], layer_part((8 * F, 8 * C), layer)),
             (kron["w2"], layer_part((8 * C, 8 * F), layer)),
@@ -505,11 +515,10 @@
     )
 
 
-def back_rows(first, layer, wire, field, kron, tabs, top=None, base=None, grads=None, y=None, slope=None):
-    args = [
+def back_rows(first, layer, wire, field, kron, tabs, slots, into, top=None, base=None, grads=None, y=None, slope=None):
+    args = [(f, full(f.shape)) for f in field] + [
         (wire, wire_part(0)),
         (tabs["eiz" if first else "ewz"], full((2, 4 * M, N))),
-        (field, full(FIELD)),
         (kron["wst"], layer_part((8 * C, 8 * C), layer)),
         (kron["w1"], layer_part((8 * F, 8 * C), layer)),
         (kron["w1t"], layer_part((8 * C, 8 * F), layer)),
@@ -529,15 +538,16 @@
         pltpu.VMEM(FIELD, F32 if first else BF),
     ]
     return call(
-        functools.partial(back_body, first, layer),
+        functools.partial(back_body, first, layer, len(field)),
         "back_rows",
         args,
         [
             FIELD_OUT,
-            (shape_of((SLABS, WIRE, LANES), BF), wire_part(0)),
+            (shape_of((SLABS, slots * WIRE, LANES), BF), wire_part(0)),
             (shape_of((F, LANES), F32), full((F, LANES))),
         ],
         scratch=scratch,
+        into=None if into is None else (1, into),
     )
 
 
@@ -576,7 +586,7 @@
     )
 
 
-def modes_back(wire, spec, layer, tabs, grads=None, slots=1):
+def modes_back(wire, spec, layer, tabs, grads=None, slots=1, into=None):
     tail = grads is not None
     rows = WIRE + (F if tail else 0)
     args = [(wire, wire_part(0)), (spec, spec_part(layer)), (tabs["col"], full(COL))]
@@ -588,6 +598,7 @@
         args,
         [(shape_of((SLABS, slots * rows, LANES), BF), wire_part(0, rows)), SPECTRUM_OUT],
         scratch=[MIXED, MIXED, HALF, HALF],
+        into=None if into is None else (0, into),
     )
 
 
@@ -603,10 +614,10 @@
         out_shape=shape_of((LAYERS, KB, 2 * C * C, LANES), F32),
         grid_spec=pltpu.PrefetchScalarGridSpec(
             num_scalar_prefetch=0,
-            grid=(KB,),
+            grid=(KB // STEP,),
             in_specs=specs,
             out_specs=pl.BlockSpec(
-                (None, None, 2 * C * C, LANES), lambda k: (layer, k, 0, 0)
+                (None, STEP, 2 * C * C, LANES), lambda k: (layer, k, 0, 0)
             ),
             scratch_shapes=[HALF, MIXED, MIXED],
         ),
@@ -622,7 +633,7 @@
         finish_body,
         "finish",
         [(wire, wire_part(0, rows)), (base, full(FIELD)), (tabs["ewz"], full((2, 4 * M, N)))],
-        [FIELD_OUT, (shape_of((F, LANES), F32), full((F, LANES)))],
+        [FIELD_OUT] + [(shape_of((2 * C, n), F32), full((2 * C, n))) for n in (F, F, C)],
         scratch=[LEFT],
     )
 
@@ -656,52 +667,55 @@
     returned = returned.reshape(FIELD)
     stash = stash.reshape(FIELD)
     spec_w = spec_w[0].transpose(0, 1, 3, 4, 2, 5).reshape(LAYERS, KB, 2 * C * C, LANES)
+    together = lax.optimization_barrier
+    kept_a = shifted(stash[: CUTS[0]], half)
     kron = prep(skip_w, up_w, down_w)
-    kept_a = shifted(stash[:EARLY], half)
-
     wire = row_dft(stash, tabs, 0, 2)
     wire = row_dft(emitted, tabs, 1, 2, into=wire)
+    wire, kept_a, kron, stash_b = together((wire, kept_a, kron, stash[CUTS[0] : CUTS[1]]))
     wire = exchange(wire)
+    kept_b = shifted(stash_b, half)
     x_0 = shifted(spectrum(wire, 0, tabs), half)
     ahead_x = shifted(spectrum(wire, 1, tabs), 1)
-    stash_b, emitted, x_0, ahead_x = lax.optimization_barrier((stash[EARLY:], emitted, x_0, ahead_x))
-    kept_b = shifted(stash_b, half)
+    stash_c, x_0, kept_b = together((stash[CUTS[1] :], x_0, kept_b))
+    kept_c = shifted(stash_c, half)
+
+    wire = mix_out(x_0, spec_w, 0, tabs, 0, 1)
+    kept_c, wire, ahead_x = together((kept_c, wire, ahead_x))
+    wire = exchange(wire)
+    kept = (kept_a, kept_b, kept_c)
+    out = mix_out(ahead_x, spec_w, 0, tabs, 1, 2)
+    emitted, returned, wire, out = together((emitted, returned, wire, out))
     ahead = shifted(emitted, 1)
-    kept = jnp.concatenate([kept_a, kept_b], axis=0)
-
-    wire = mix_out(x_0, spec_w, 0, tabs, 0, 2)
-    wire = mix_out(ahead_x, spec_w, 0, tabs, 1, 2, into=wire)
-    first_wire = exchange(wire)
-    kept_1, out, y_0, slope_0 = forward_rows(first_wire, 0, kept, kron, 0, tabs, True, False)
-    returned, out = lax.optimization_barrier((returned, out))
+    top = shifted(returned, -1)
+    kept_1, out, y_0, slope_0 = forward_rows(wire, 0, kept, kron, 0, tabs, True, False, 0, 2, into=out)
+    second = exchange(out)
+    x_1, out = modes(second, 0, spec_w, 1, tabs, 0, 1)
     wire = exchange(out)
-    top = shifted(returned, -1)
-    x_1, out = modes(wire, 0, spec_w, 1, tabs, 0, 2)
-    ahead_1, out = forward_rows(first_wire, 1, ahead, kron, 0, tabs, False, False, 1, 2, into=out)
-    second_wire = exchange(out)
-
-    base, out, grads = back_rows(True, 1, second_wire, kept_1, kron, tabs, top=top)
+    ahead_1, out = forward_rows(second, 1, (ahead,), kron, 0, tabs, False, False, 1, 2)
+    wire, ahead_1, out = together((wire, ahead_1, out))
+
+    base, out, grads = back_rows(True, 1, wire, (kept_1,), kron, tabs, 2, out, top=top)
+    third = exchange(out)
+    out, gy_1 = modes_back(third, spec_w, 1, tabs)
     wire = exchange(out)
-    out, gy_1 = modes_back(wire, spec_w, 1, tabs, slots=2)
-    _, out = modes(second_wire, 1, spec_w, 1, tabs, 1, 2, into=out)
-    third_wire = exchange(out)
+    _, out = modes(third, 1, spec_w, 1, tabs, 1, 2)
+    wire, out = together((wire, out))
+    base, out, grads = back_rows(
+        False, 0, wire, kept, kron, tabs, 2, out, base=base, grads=grads, y=y_0, slope=slope_0
+    )
+    fourth = exchange(out)
     grad_spec = spec_grad(gy_1, x_1, 1)
-    base, out, grads = back_rows(
-        False, 0, third_wire, kept, kron, tabs, base=base, grads=grads, y=y_0, slope=slope_0
-    )
-    wire = exchange(out)
-    (sent,) = forward_rows(third_wire, 1, ahead_1, kron, 1, tabs, False, True)
-    out, gy_0 = modes_back(wire, spec_w, 0, tabs, grads)
+    fourth, grad_spec = together((fourth, grad_spec))
+    out, gy_0 = modes_back(fourth, spec_w, 0, tabs, grads)
     wire = exchange(out)
     grad_spec = spec_grad(gy_0, x_0, 0, into=grad_spec)
-    back_grad, packed = finish(wire, base, tabs)
-
-    def slot(number):
-        return jnp.stack([packed[:, (number * 2 + l) * C : (number * 2 + l + 1) * C] for l in range(LAYERS)])
-
-    grad_down = jnp.swapaxes(slot(0), 1, 2)
-    grad_up = slot(1)
-    grad_skip = slot(2)[:, :C]
+    (sent,) = forward_rows(fourth, 1, (ahead_1,), kron, 1, tabs, False, True)
+    wire, grad_spec, sent = together((wire, grad_spec, sent))
+    back_grad, grad_down, grad_up, grad_skip = finish(wire, base, tabs)
+    grad_skip = grad_skip.reshape(C, LAYERS, C).transpose(1, 0, 2)
+    grad_up = grad_up.reshape(C, LAYERS, F).transpose(1, 2, 0)
+    grad_down = grad_down.reshape(C, LAYERS, F).transpose(1, 0, 2)
     field = (1, C, ROWS, N)
     return (
         sent.reshape(field),

time: 240 us -> 215 us (0.90)
  blocking collectives: 64.4 us -> 28.6 us
  starting transfers between devices: 24.1 us -> 48.7 us
  waiting for transfers between devices: 32.7 us -> 24.1 us
  local copies, waits for them, and re-layouts: 12.3 us -> 9.46 us
    all_to_all x5 -> x2, blocking collectives: 64.4 us -> 28.6 us  [exchange(): return lax.all_to_all(wire, 'slab', split_axis=0, concat_axis=0, tiled=True)]
    ppermute x6 -> x7, waiting for transfers between devices: 27.4 us -> 10 us  [shifted(): lax.ppermute(block, 'section', [(i, (i + distance) % count) for i in rang...]
    all_to_all x3 -> x6, starting transfers between devices: 16.7 us -> 29.8 us  [exchange(): return lax.all_to_all(wire, 'slab', split_axis=0, concat_axis=0, tiled=True)]
    ppermute x6 -> x7, starting transfers between devices: 7.41 us -> 18.9 us  [shifted(): lax.ppermute(block, 'section', [(i, (i + distance) % count) for i in rang...]
    all_to_all x3 -> x6, waiting for transfers between devices: 5.25 us -> 14 us  [exchange(): return lax.all_to_all(wire, 'slab', split_axis=0, concat_axis=0, tiled=True)]
    pallas_call x2, Pallas kernels: 8.62 us -> 5.72 us  [spec_grad(): pl.pallas_call(body, out_shape=shape_of((LAYERS, KB, 2 * C * C, LANES), F...]
    unnamed x29 -> x35, local copies, waits for them, and re-layouts: 8.29 us -> 6.31 us
  transfers between devices with their start and end apart: 9 -> 13, of which waited for: 3 -> 8; matrix products, arithmetic and copies ran while one was open for 2% -> 2% of each run, Pallas kernels for 22% -> 28%
where the time goes in v1:
time: 215 us; the launch traced here: 212 us
  Pallas kernels  101 us (47%)
  starting transfers between devices  48.7 us (23%)
  blocking collectives  28.6 us (13%)
  waiting for transfers between devices  24.1 us (11%)
  local copies, waits for them, and re-layouts  9.46 us (4%)
    pallas_call x17, Pallas kernels, call(): pl.pallas_call(body, out_shape=[o for o, _ in outs], grid_spec=pltpu.Pref...  94.9 us
    all_to_all x6, starting transfers between devices, exchange(): return lax.all_to_all(wire, 'slab', split_axis=0, concat_axis=0, tiled=True)  29.8 us
    all_to_all x2, blocking collectives, exchange(): return lax.all_to_all(wire, 'slab', split_axis=0, concat_axis=0, tiled=True)  28.6 us
    ppermute x7, starting transfers between devices, shifted(): lax.ppermute(block, 'section', [(i, (i + distance) % count) for i in rang...  18.9 us
    all_to_all x6, waiting for transfers between devices, exchange(): return lax.all_to_all(wire, 'slab', split_axis=0, concat_axis=0, tiled=True)  14 us
    ppermute x7, waiting for transfers between devices, shifted(): lax.ppermute(block, 'section', [(i, (i + distance) % count) for i in rang...  10 us
    unnamed x35, local copies, waits for them, and re-layouts  6.31 us
    pallas_call x2, Pallas kernels, spec_grad(): pl.pallas_call(body, out_shape=shape_of((LAYERS, KB, 2 * C * C, LANES), F...  5.72 us
  transfers between devices with their start and end apart: 13, of which 8 were waited for; matrix products, arithmetic and copies ran while one was open for 2% of the time, Pallas kernels for 28%

profile of v1, /device:TPU:2, one launch (start us, length us, event | category | flops | bytes accessed | tf_op | source)
XLA Modules:
  0.0 212.1 jit_solution(11871398370179403199)
XLA Ops:
  1.8 4.0 %collective-permute-start = (bf16[5,2,64,512]{3,2,1,0:T(8,128)(2,1)S(1)}, bf16[5,2,64,512]{3,2,1,0:T(8,128)(2,1)S(1)}, u32[]{:S(2)}, u32[]{:S(2)}) collective-permute-start(bf16[5,2,64,512]{3,2,1,0:T(8,128)(2,1)S(1)} %bitcast.44), channel_id=1, source_target_pairs={{0,64},{8,72},{16,80},{24,88},{32,96},{40,104},{48,112},{56,120},{... | collective-permute-start | bytes 1966088 | tf_op jit(solution)/shard_map/ppermute | solution.py:660
  20.5 5.6 %all-to-all-start = ((bf16[8,320,128]{2,1,0:T(8,128)(2,1)}), bf16[8,320,128]{2,1,0:T(8,128)(2,1)S(1)}, u32[]{:S(2)}, u32[]{:S(2)}) async-start(bf16[8,320,128]{2,1,0:T(8,128)(2,1)} %row_dft.3), calls=%async_computation | async-start | bytes 1310720 | tf_op jit(solution)/shard_map/all_to_all | solution.py:655
  26.1 3.6 %collective-permute-start.2 = (bf16[3,2,64,512]{3,2,1,0:T(8,128)(2,1)S(1)}, bf16[3,2,64,512]{3,2,1,0:T(8,128)(2,1)S(1)}, u32[]{:S(2)}, u32[]{:S(2)}) collective-permute-start(bf16[3,2,64,512]{3,2,1,0:T(8,128)(2,1)S(1)} %bitcast.45), channel_id=1, source_target_pairs={{0,64},{8,72},{16,80},{24,88},{32,96},{40,104},{48,112},{56,120},{... | collective-permute-start | bytes 1179656 | tf_op jit(solution)/shard_map/ppermute | solution.py:660
  29.7 6.0 %all-to-all-done.recv_ref = bf16[8,320,128]{2,1,0:T(8,128)(2,1)S(1)} async-done(((bf16[8,320,128]{2,1,0:T(8,128)(2,1)}), bf16[8,320,128]{2,1,0:T(8,128)(2,1)S(1)}, u32[]{:S(2)}, u32[]{:S(2)}) %all-to-all-start) | async-done | bytes 655392 | tf_op jit(solution)/shard_map/all_to_all | solution.py:655
  38.5 3.7 %collective-permute-start.1 = (bf16[160,256]{1,0:T(8,128)(2,1)}, bf16[160,256]{1,0:T(8,128)(2,1)S(1)}, u32[]{:S(2)}, u32[]{:S(2)}) collective-permute-start(bf16[160,256]{1,0:T(8,128)(2,1)} %spectrum.2), channel_id=1, source_target_pairs={{0,64},{8,72},{16,80},{24,88},{32,96},{40,104},{48,112},{56,120},{... | collective-permute-start | bytes 245768 | tf_op jit(solution)/shard_map/ppermute | solution.py:660
  53.9 4.2 %collective-permute-done.4.x_ref = bf16[160,256]{1,0:T(8,128)(2,1)S(1)} collective-permute-done((bf16[160,256]{1,0:T(8,128)(2,1)}, bf16[160,256]{1,0:T(8,128)(2,1)S(1)}, u32[]{:S(2)}, u32[]{:S(2)}) %collective-permute-start.4) | collective-permute-done | bytes 81952 | tf_op jit(solution)/shard_map/ppermute | solution.py:660
  58.2 4.6 %all-to-all-start.1 = ((bf16[8,160,128]{2,1,0:T(8,128)(2,1)}), bf16[8,160,128]{2,1,0:T(8,128)(2,1)S(1)}, u32[]{:S(2)}, u32[]{:S(2)}) async-start(bf16[8,160,128]{2,1,0:T(8,128)(2,1)} %mix_out.2), calls=%async_computation.1 | async-start | bytes 655360 | tf_op jit(solution)/shard_map/all_to_all | solution.py:655
  68.4 5.4 %collective-permute-start.6 = (bf16[10,2,64,512]{3,2,1,0:T(8,128)(2,1)}, bf16[10,2,64,512]{3,2,1,0:T(8,128)(2,1)S(1)}, u32[]{:S(2)}, u32[]{:S(2)}) collective-permute-start(bf16[10,2,64,512]{3,2,1,0:T(8,128)(2,1)} %bitcast.47), channel_id=1, source_target_pairs={{0,120},{8,0},{16,8},{24,16},{32,24},{40,32},{48,40},{56,48},{64,5... | collective-permute-start | bytes 3932168 | tf_op jit(solution)/shard_map/ppermute | solution.py:660
  73.7 9.1 %forward_rows.3 = (bf16[10,2,64,512]{3,2,1,0:T(8,128)(2,1)}, bf16[8,320,128]{2,1,0:T(8,128)(2,1)}, bf16[10,2,64,512]{3,2,1,0:T(8,128)(2,1)}, bf16[10,2,64,512]{3,2,1,0:T(8,128)(2,1)}) custom-call(bf16[5,2,64,512]{3,2,1,0:T(8,128)(2,1)} %copy-done.2, bf16[3,2,64,512]{3,2,1,0:T(8,128)(2,1)} %copy-done.4, ...), custom_call_target="tpu_custom_call", output_to_operand_aliasing={{1}: (9, {})} | custom-call | tf_op jit(solution)/shard_map/forward_rows/pallas_call | solution.py:463
  82.8 13.5 %all_to_all.40.recv_ref.refs_1_ = bf16[8,320,128]{2,1,0:T(8,128)(2,1)} all-to-all(bf16[8,320,128]{2,1,0:T(8,128)(2,1)} %get-tuple-element.85), channel_id=1, replica_groups=mesh['section'=16,'slab'=8] {'slab'}, dimensions={0} | all-to-all | bytes 1310720 | tf_op jit(solution)/shard_map/all_to_all | solution.py:655
  96.3 4.1 %modes.2 = (bf16[160,256]{1,0:T(8,128)(2,1)}, bf16[8,160,128]{2,1,0:T(8,128)(2,1)}) custom-call(bf16[8,320,128]{2,1,0:T(8,128)(2,1)} %all_to_all.40.recv_ref.refs_1_, bf16[2,8,800,128]{3,2,1,0:T(8,128)(2,1)} %bitcast.35, bf16[8,128,256]{2,1,0:T(8,128)(2,1)} %constant.14.clone.col_ref.refs_2_), custom_call_target="tpu_custom_call" | custom-call | tf_op jit(solution)/shard_map/modes/pallas_call | solution.py:463
  100.5 4.9 %all-to-all-start.3 = ((bf16[8,160,128]{2,1,0:T(8,128)(2,1)}), bf16[8,160,128]{2,1,0:T(8,128)(2,1)S(1)}, u32[]{:S(2)}, u32[]{:S(2)}) async-start(bf16[8,160,128]{2,1,0:T(8,128)(2,1)} %get-tuple-element.86), calls=%async_computation.3 | async-start | bytes 655360 | tf_op jit(solution)/shard_map/all_to_all | solution.py:655
  105.3 8.0 %forward_rows.4 = (bf16[10,2,64,512]{3,2,1,0:T(8,128)(2,1)}, bf16[8,320,128]{2,1,0:T(8,128)(2,1)}) custom-call(bf16[10,2,64,512]{3,2,1,0:T(8,128)(2,1)} %collective-permute-done.5.refs_0_, bf16[8,320,128]{2,1,0:T(8,128)(2,1)} %all_to_all.40.recv_ref.refs_1_, bf16[2,160,160]{2,1,0:T(8,128)(2,1)} %get-tuple-element.80.refs_4_.refs_2_.refs_9_, ...), custom_call_target="tpu_custom_call" | custom-call | tf_op jit(solution)/shard_map/forward_rows/pallas_call | solution.py:463
  114.5 15.3 %back_rows.2 = (bf16[10,2,64,512]{3,2,1,0:T(8,128)(2,1)}, bf16[8,320,128]{2,1,0:T(8,128)(2,1)}, f32[80,128]{1,0:T(8,128)}) custom-call(bf16[10,2,64,512]{3,2,1,0:T(8,128)(2,1)} %get-tuple-element.84.refs_0_, bf16[8,160,128]{2,1,0:T(8,128)(2,1)} %copy-done.6, ...), custom_call_target="tpu_custom_call", output_to_operand_aliasing={{1}: (10, {})} | custom-call | tf_op jit(solution)/shard_map/back_rows/pallas_call | solution.py:463
  129.8 15.0 %all_to_all.41.refs_0_.recv_ref = bf16[8,320,128]{2,1,0:T(8,128)(2,1)} all-to-all(bf16[8,320,128]{2,1,0:T(8,128)(2,1)} %get-tuple-element.96), channel_id=1, replica_groups=mesh['section'=16,'slab'=8] {'slab'}, dimensions={0} | all-to-all | bytes 1310720 | tf_op jit(solution)/shard_map/all_to_all | solution.py:655
  144.8 4.0 %modes_back.2 = (bf16[8,160,128]{2,1,0:T(8,128)(2,1)}, bf16[160,256]{1,0:T(8,128)(2,1)}) custom-call(bf16[8,320,128]{2,1,0:T(8,128)(2,1)} %all_to_all.41.refs_0_.recv_ref, bf16[2,8,800,128]{3,2,1,0:T(8,128)(2,1)} %bitcast.36, bf16[8,128,256]{2,1,0:T(8,128)(2,1)} %constant.14.clone.col_ref.refs_2_), custom_call_target="tpu_custom_call" | custom-call | tf_op jit(solution)/shard_map/modes_back/pallas_call | solution.py:463
  148.9 4.9 %all-to-all-start.5 = ((bf16[8,160,128]{2,1,0:T(8,128)(2,1)}), bf16[8,160,128]{2,1,0:T(8,128)(2,1)S(1)}, u32[]{:S(2)}, u32[]{:S(2)}) async-start(bf16[8,160,128]{2,1,0:T(8,128)(2,1)} %get-tuple-element.97), calls=%async_computation.5 | async-start | bytes 655360 | tf_op jit(solution)/shard_map/all_to_all | solution.py:655
  153.7 4.1 %modes.3 = (bf16[160,256]{1,0:T(8,128)(2,1)}, bf16[8,320,128]{2,1,0:T(8,128)(2,1)}) custom-call(bf16[8,320,128]{2,1,0:T(8,128)(2,1)} %all_to_all.41.refs_0_.recv_ref, bf16[2,8,800,128]{3,2,1,0:T(8,128)(2,1)} %bitcast.37, bf16[8,128,256]{2,1,0:T(8,128)(2,1)} %constant.14.clone.col_ref.refs_2_), custom_call_target="tpu_custom_call" | custom-call | tf_op jit(solution)/shard_map/modes/pallas_call | solution.py:463
  160.1 15.1 %back_rows.3 = (bf16[10,2,64,512]{3,2,1,0:T(8,128)(2,1)}, bf16[8,320,128]{2,1,0:T(8,128)(2,1)}, f32[80,128]{1,0:T(8,128)}) custom-call(bf16[5,2,64,512]{3,2,1,0:T(8,128)(2,1)} %copy-done.2, bf16[3,2,64,512]{3,2,1,0:T(8,128)(2,1)} %copy-done.4, bf16[2,2,64,512]{3,2,1,0:T(8,128)(2,1)} %copy-done.10, ...), custom_call_target="tpu_custom_call", output_to_operand_aliasing={{1}: (14, {})} | custom-call | tf_op jit(solution)/shard_map/back_rows/pallas_call | solution.py:463
  175.2 5.1 %all-to-all-start.6 = ((bf16[8,320,128]{2,1,0:T(8,128)(2,1)}), bf16[8,320,128]{2,1,0:T(8,128)(2,1)S(1)}, u32[]{:S(2)}, u32[]{:S(2)}) async-start(bf16[8,320,128]{2,1,0:T(8,128)(2,1)} %get-tuple-element.105), calls=%async_computation.6 | async-start | bytes 1310720 | tf_op jit(solution)/shard_map/all_to_all | solution.py:655
  183.1 4.6 %all-to-all-done.6.refs_0_.refs_1_ = bf16[8,320,128]{2,1,0:T(8,128)(2,1)S(1)} async-done(((bf16[8,320,128]{2,1,0:T(8,128)(2,1)}), bf16[8,320,128]{2,1,0:T(8,128)(2,1)S(1)}, u32[]{:S(2)}, u32[]{:S(2)}) %all-to-all-start.6) | async-done | bytes 655392 | tf_op jit(solution)/shard_map/all_to_all | solution.py:655
  188.6 4.1 %modes_back.3 = (bf16[8,240,128]{2,1,0:T(8,128)(2,1)}, bf16[160,256]{1,0:T(8,128)(2,1)}) custom-call(bf16[8,320,128]{2,1,0:T(8,128)(2,1)} %copy-done, bf16[2,8,800,128]{3,2,1,0:T(8,128)(2,1)} %bitcast.38, bf16[8,128,256]{2,1,0:T(8,128)(2,1)} %constant.14.clone.col_ref.refs_2_, f32[80,128]{1,0:T(8,128)} %get-tuple-element.109.refs_3_), custom_call_target="tpu_custom_call" | custom-call | tf_op jit(solution)/shard_map/modes_back/pallas_call | solution.py:463
  192.7 4.8 %all-to-all-start.7 = ((bf16[8,240,128]{2,1,0:T(8,128)(2,1)}), bf16[8,240,128]{2,1,0:T(8,128)(2,1)S(1)}, u32[]{:S(2)}, u32[]{:S(2)}) async-start(bf16[8,240,128]{2,1,0:T(8,128)(2,1)} %get-tuple-element.110), calls=%async_computation.7 | async-start | bytes 983040 | tf_op jit(solution)/shard_map/all_to_all | solution.py:655
  197.5 7.7 %forward_rows.5 = bf16[10,2,64,512]{3,2,1,0:T(8,128)(2,1)} custom-call(bf16[10,2,64,512]{3,2,1,0:T(8,128)(2,1)} %get-tuple-element.113.refs_0_, bf16[8,320,128]{2,1,0:T(8,128)(2,1)} %copy-done, bf16[2,160,160]{2,1,0:T(8,128)(2,1)} %get-tuple-element.80.refs_4_.refs_2_.refs_9_, bf16[2,640,160]{2,1,0:T(8,128)(2,1)} %get-tuple-element.81.refs_5_.refs_3_.refs_4_.refs_6_, ...), custom_call_target="tpu_custom_call" | custom-call | tf_op jit(solution)/shard_map/forward_rows/pallas_call | solution.py:463
  (61 shorter events, 50.1 us)
Async XLA Ops:
  0.6 6.2 %copy-start.13 = (bf16[1,2,20,20]{3,1,2,0:T(2,128)(2,1)S(1)}, bf16[1,2,20,20]{3,1,2,0:T(2,128)(2,1)}, u32[]{:S(2)}) copy-start(bf16[1,2,20,20]{3,1,2,0:T(2,128)(2,1)} %param.15) | copy-start | bytes 4804
  0.6 6.8 %copy-start.14 = (bf16[1,2,20,80]{3,1,2,0:T(2,128)(2,1)S(1)}, bf16[1,2,20,80]{3,1,2,0:T(2,128)(2,1)}, u32[]{:S(2)}) copy-start(bf16[1,2,20,80]{3,1,2,0:T(2,128)(2,1)} %param.17) | copy-start | bytes 19204
  0.7 7.4 %copy-start.15 = (bf16[1,2,80,20]{2,1,3,0:T(2,128)(2,1)S(1)}, bf16[1,2,80,20]{2,1,3,0:T(2,128)(2,1)}, u32[]{:S(2)}) copy-start(bf16[1,2,80,20]{2,1,3,0:T(2,128)(2,1)} %param.16) | copy-start | bytes 19204
  1.8 18.7 %collective-permute-start = (bf16[5,2,64,512]{3,2,1,0:T(8,128)(2,1)S(1)}, bf16[5,2,64,512]{3,2,1,0:T(8,128)(2,1)S(1)}, u32[]{:S(2)}, u32[]{:S(2)}) collective-permute-start(bf16[5,2,64,512]{3,2,1,0:T(8,128)(2,1)S(1)} %bitcast.44), channel_id=1, source_target_pairs={{0,64},{8,72},{16,80},{24,88},{32,96},{40,104},{48,112},{56,120},{... | collective-permute-start | bytes 1966088 | tf_op jit(solution)/shard_map/ppermute | solution.py:660
  20.5 22.7 %copy-start.2 = (bf16[5,2,64,512]{3,2,1,0:T(8,128)(2,1)}, bf16[5,2,64,512]{3,2,1,0:T(8,128)(2,1)S(1)}, u32[]{:S(2)}) copy-start(bf16[5,2,64,512]{3,2,1,0:T(8,128)(2,1)S(1)} %collective-permute-done.refs_0_) | copy-start | bytes 1966084
  20.5 15.1 %all-to-all-start = ((bf16[8,320,128]{2,1,0:T(8,128)(2,1)}), bf16[8,320,128]{2,1,0:T(8,128)(2,1)S(1)}, u32[]{:S(2)}, u32[]{:S(2)}) async-start(bf16[8,320,128]{2,1,0:T(8,128)(2,1)} %row_dft.3), calls=%async_computation | async-start | bytes 1310720 | tf_op jit(solution)/shard_map/all_to_all | solution.py:655
  26.1 18.8 %collective-permute-start.2 = (bf16[3,2,64,512]{3,2,1,0:T(8,128)(2,1)S(1)}, bf16[3,2,64,512]{3,2,1,0:T(8,128)(2,1)S(1)}, u32[]{:S(2)}, u32[]{:S(2)}) collective-permute-start(bf16[3,2,64,512]{3,2,1,0:T(8,128)(2,1)S(1)} %bitcast.45), channel_id=1, source_target_pairs={{0,64},{8,72},{16,80},{24,88},{32,96},{40,104},{48,112},{56,120},{... | collective-permute-start | bytes 1179656 | tf_op jit(solution)/shard_map/ppermute | solution.py:660
  38.5 7.5 %collective-permute-start.1 = (bf16[160,256]{1,0:T(8,128)(2,1)}, bf16[160,256]{1,0:T(8,128)(2,1)S(1)}, u32[]{:S(2)}, u32[]{:S(2)}) collective-permute-start(bf16[160,256]{1,0:T(8,128)(2,1)} %spectrum.2), channel_id=1, source_target_pairs={{0,64},{8,72},{16,80},{24,88},{32,96},{40,104},{48,112},{56,120},{... | collective-permute-start | bytes 245768 | tf_op jit(solution)/shard_map/ppermute | solution.py:660
  44.9 9.0 %copy-start.4 = (bf16[3,2,64,512]{3,2,1,0:T(8,128)(2,1)}, bf16[3,2,64,512]{3,2,1,0:T(8,128)(2,1)S(1)}, u32[]{:S(2)}) copy-start(bf16[3,2,64,512]{3,2,1,0:T(8,128)(2,1)S(1)} %collective-permute-done.2.refs_1_) | copy-start | bytes 1179652
  46.0 4.4 %copy-start.11 = (bf16[160,256]{1,0:T(8,128)(2,1)}, bf16[160,256]{1,0:T(8,128)(2,1)S(1)}, u32[]{:S(2)}) copy-start(bf16[160,256]{1,0:T(8,128)(2,1)S(1)} %collective-permute-done.1.x_ref) | copy-start | bytes 245764
  46.0 12.1 %collective-permute-start.3 = (bf16[2,2,64,512]{3,2,1,0:T(8,128)(2,1)S(1)}, bf16[2,2,64,512]{3,2,1,0:T(8,128)(2,1)S(1)}, u32[]{:S(2)}, u32[]{:S(2)}) collective-permute-start(bf16[2,2,64,512]{3,2,1,0:T(8,128)(2,1)S(1)} %bitcast.46), channel_id=1, source_target_pairs={{0,64},{8,72},{16,80},{24,88},{32,96},{40,104},{48,112},{56,120},{... | collective-permute-start | bytes 786440 | tf_op jit(solution)/shard_map/ppermute | solution.py:660
  50.5 7.7 %collective-permute-start.4 = (bf16[160,256]{1,0:T(8,128)(2,1)}, bf16[160,256]{1,0:T(8,128)(2,1)S(1)}, u32[]{:S(2)}, u32[]{:S(2)}) collective-permute-start(bf16[160,256]{1,0:T(8,128)(2,1)} %spectrum.3), channel_id=1, source_target_pairs={{0,8},{8,16},{16,24},{24,32},{32,40},{40,48},{48,56},{56,64},{64,7... | collective-permute-start | bytes 245768 | tf_op jit(solution)/shard_map/ppermute | solution.py:660
  58.2 4.6 %copy-start.12 = (bf16[160,256]{1,0:T(8,128)(2,1)}, bf16[160,256]{1,0:T(8,128)(2,1)S(1)}, u32[]{:S(2)}) copy-start(bf16[160,256]{1,0:T(8,128)(2,1)S(1)} %collective-permute-done.4.x_ref) | copy-start | bytes 245764
  58.2 8.2 %copy-start.10 = (bf16[2,2,64,512]{3,2,1,0:T(8,128)(2,1)}, bf16[2,2,64,512]{3,2,1,0:T(8,128)(2,1)S(1)}, u32[]{:S(2)}) copy-start(bf16[2,2,64,512]{3,2,1,0:T(8,128)(2,1)S(1)} %collective-permute-done.3.refs_2_) | copy-start | bytes 786436
  58.2 10.2 %all-to-all-start.1 = ((bf16[8,160,128]{2,1,0:T(8,128)(2,1)}), bf16[8,160,128]{2,1,0:T(8,128)(2,1)S(1)}, u32[]{:S(2)}, u32[]{:S(2)}) async-start(bf16[8,160,128]{2,1,0:T(8,128)(2,1)} %mix_out.2), calls=%async_computation.1 | async-start | bytes 655360 | tf_op jit(solution)/shard_map/all_to_all | solution.py:655
  62.7 5.6 %copy-start.8 = (bf16[1,20,64,512]{3,2,1,0:T(8,128)(2,1)S(1)}, bf16[1,20,64,512]{3,2,1,0:T(8,128)(2,1)}, u32[]{:S(2)}) copy-start(bf16[1,20,64,512]{3,2,1,0:T(8,128)(2,1)} %param.12) | copy-start | bytes 3932164
  68.3 5.4 %copy-start.7 = (bf16[8,160,128]{2,1,0:T(8,128)(2,1)}, bf16[8,160,128]{2,1,0:T(8,128)(2,1)S(1)}, u32[]{:S(2)}) copy-start(bf16[8,160,128]{2,1,0:T(8,128)(2,1)S(1)} %all-to-all-done.1.refs_3_) | copy-start | bytes 983044
  68.3 37.0 %collective-permute-start.5 = (bf16[10,2,64,512]{3,2,1,0:T(8,128)(2,1)S(1)}, bf16[10,2,64,512]{3,2,1,0:T(8,128)(2,1)}, u32[]{:S(2)}, u32[]{:S(2)}) collective-permute-start(bf16[10,2,64,512]{3,2,1,0:T(8,128)(2,1)S(1)} %bitcast.43), channel_id=1, source_target_pairs={{0,8},{8,16},{16,24},{24,32},{32,40},{40,48},{48,56},{56,64},{64,7... | collective-permute-start | bytes 3932168 | tf_op jit(solution)/shard_map/ppermute | solution.py:660
  68.4 45.0 %collective-permute-start.6 = (bf16[10,2,64,512]{3,2,1,0:T(8,128)(2,1)}, bf16[10,2,64,512]{3,2,1,0:T(8,128)(2,1)S(1)}, u32[]{:S(2)}, u32[]{:S(2)}) collective-permute-start(bf16[10,2,64,512]{3,2,1,0:T(8,128)(2,1)} %bitcast.47), channel_id=1, source_target_pairs={{0,120},{8,0},{16,8},{24,16},{32,24},{40,32},{48,40},{56,48},{64,5... | collective-permute-start | bytes 3932168 | tf_op jit(solution)/shard_map/ppermute | solution.py:660
  100.5 12.9 %all-to-all-start.3 = ((bf16[8,160,128]{2,1,0:T(8,128)(2,1)}), bf16[8,160,128]{2,1,0:T(8,128)(2,1)S(1)}, u32[]{:S(2)}, u32[]{:S(2)}) async-start(bf16[8,160,128]{2,1,0:T(8,128)(2,1)} %get-tuple-element.86), calls=%async_computation.3 | async-start | bytes 655360 | tf_op jit(solution)/shard_map/all_to_all | solution.py:655
  113.3 1.2 copy-start.9
  148.9 10.5 %all-to-all-start.5 = ((bf16[8,160,128]{2,1,0:T(8,128)(2,1)}), bf16[8,160,128]{2,1,0:T(8,128)(2,1)S(1)}, u32[]{:S(2)}, u32[]{:S(2)}) async-start(bf16[8,160,128]{2,1,0:T(8,128)(2,1)} %get-tuple-element.97), calls=%async_computation.5 | async-start | bytes 655360 | tf_op jit(solution)/shard_map/all_to_all | solution.py:655
  175.2 12.6 %all-to-all-start.6 = ((bf16[8,320,128]{2,1,0:T(8,128)(2,1)}), bf16[8,320,128]{2,1,0:T(8,128)(2,1)S(1)}, u32[]{:S(2)}, u32[]{:S(2)}) async-start(bf16[8,320,128]{2,1,0:T(8,128)(2,1)} %get-tuple-element.105), calls=%async_computation.6 | async-start | bytes 1310720 | tf_op jit(solution)/shard_map/all_to_all | solution.py:655
  192.7 15.4 %all-to-all-start.7 = ((bf16[8,240,128]{2,1,0:T(8,128)(2,1)}), bf16[8,240,128]{2,1,0:T(8,128)(2,1)S(1)}, u32[]{:S(2)}, u32[]{:S(2)}) async-start(bf16[8,240,128]{2,1,0:T(8,128)(2,1)} %get-tuple-element.110), calls=%async_computation.7 | async-start | bytes 983040 | tf_op jit(solution)/shard_map/all_to_all | solution.py:655
  (5 other events, 4.0 us)

commit v2 on v1

--- a/solution.py
+++ b/solution.py
@@ -262,17 +262,20 @@
 
 def to_spectrum(recv_ref, col_ref):
     total = jnp.zeros((WIRE, 4 * M), F32)
-    for j in range(SLABS):
-        total = total + dot(recv_ref[j], col_ref[j])
+    for j in range(0, SLABS, 2):
+        pair = jnp.concatenate([recv_ref[j], recv_ref[j + 1]], axis=1)
+        total = total + dot(pair, col_ref[j : j + 2].reshape(4 * ROWS, 4 * M))
     return total
 
 
 def from_spectrum(values, col_ref, send_ref, scale):
-    for j in range(SLABS):
-        r = dot_nt(values, col_ref[j])
+    for j in range(0, SLABS, 2):
+        r = dot_nt(values, col_ref[j : j + 2].reshape(4 * ROWS, 4 * M))
         if scale != 1.0:
             r = r * scale
-        send_ref[j, 0:WIRE, :] = r.astype(BF)
+        r = r.astype(BF)
+        send_ref[j, 0:WIRE, :] = r[:, :LANES]
+        send_ref[j + 1, 0:WIRE, :] = r[:, LANES:]
 
 
 def spectrum_in(ref, value):
@@ -419,7 +422,8 @@
 
 
 FIELD = (CP, 2, ROWS, N)
-LIMIT = pltpu.CompilerParams(vmem_limit_bytes=60 * 1024 * 1024)
+MIB = 1024 * 1024
+LIMIT = pltpu.CompilerParams(vmem_limit_bytes=60 * MIB)
 
 
 def full(shape):

time: 215 us -> 214 us (level)
  no operation moved by 1% of the time
where the time goes in v2:
time: 214 us; the launch traced here: 211 us
  Pallas kernels  99.4 us (46%)
  starting transfers between devices  48.6 us (23%)
  blocking collectives  28.6 us (13%)
  waiting for transfers between devices  24.4 us (11%)
  local copies, waits for them, and re-layouts  9.46 us (4%)
    pallas_call x17, Pallas kernels, call(): pl.pallas_call(body, out_shape=[o for o, _ in outs], grid_spec=pltpu.Pref...  93.7 us
    all_to_all x6, starting transfers between devices, exchange(): return lax.all_to_all(wire, 'slab', split_axis=0, concat_axis=0, tiled=True)  29.8 us
    all_to_all x2, blocking collectives, exchange(): return lax.all_to_all(wire, 'slab', split_axis=0, concat_axis=0, tiled=True)  28.6 us
    ppermute x7, starting transfers between devices, shifted(): lax.ppermute(block, 'section', [(i, (i + distance) % count) for i in rang...  18.8 us
    all_to_all x6, waiting for transfers between devices, exchange(): return lax.all_to_all(wire, 'slab', split_axis=0, concat_axis=0, tiled=True)  14.3 us
    ppermute x7, waiting for transfers between devices, shifted(): lax.ppermute(block, 'section', [(i, (i + distance) % count) for i in rang...  10.1 us
    unnamed x35, local copies, waits for them, and re-layouts  6.31 us
    pallas_call x2, Pallas kernels, spec_grad(): pl.pallas_call(body, out_shape=shape_of((LAYERS, KB, 2 * C * C, LANES), F...  5.72 us
  transfers between devices with their start and end apart: 13, of which 8 were waited for; matrix products, arithmetic and copies ran while one was open for 2% of the time, Pallas kernels for 28%

profile of v2, /device:TPU:2, one launch (start us, length us, event | category | flops | bytes accessed | tf_op | source)
XLA Modules:
  0.0 211.2 jit_solution(16075663146712089945)
XLA Ops:
  1.8 4.0 %collective-permute-start = (bf16[5,2,64,512]{3,2,1,0:T(8,128)(2,1)S(1)}, bf16[5,2,64,512]{3,2,1,0:T(8,128)(2,1)S(1)}, u32[]{:S(2)}, u32[]{:S(2)}) collective-permute-start(bf16[5,2,64,512]{3,2,1,0:T(8,128)(2,1)S(1)} %bitcast.44), channel_id=1, source_target_pairs={{0,64},{8,72},{16,80},{24,88},{32,96},{40,104},{48,112},{56,120},{... | collective-permute-start | bytes 1966088 | tf_op jit(solution)/shard_map/ppermute | solution.py:664
  20.5 5.6 %all-to-all-start = ((bf16[8,320,128]{2,1,0:T(8,128)(2,1)}), bf16[8,320,128]{2,1,0:T(8,128)(2,1)S(1)}, u32[]{:S(2)}, u32[]{:S(2)}) async-start(bf16[8,320,128]{2,1,0:T(8,128)(2,1)} %row_dft.3), calls=%async_computation | async-start | bytes 1310720 | tf_op jit(solution)/shard_map/all_to_all | solution.py:659
  26.1 3.6 %collective-permute-start.2 = (bf16[3,2,64,512]{3,2,1,0:T(8,128)(2,1)S(1)}, bf16[3,2,64,512]{3,2,1,0:T(8,128)(2,1)S(1)}, u32[]{:S(2)}, u32[]{:S(2)}) collective-permute-start(bf16[3,2,64,512]{3,2,1,0:T(8,128)(2,1)S(1)} %bitcast.45), channel_id=1, source_target_pairs={{0,64},{8,72},{16,80},{24,88},{32,96},{40,104},{48,112},{56,120},{... | collective-permute-start | bytes 1179656 | tf_op jit(solution)/shard_map/ppermute | solution.py:664
  29.7 6.0 %all-to-all-done.recv_ref = bf16[8,320,128]{2,1,0:T(8,128)(2,1)S(1)} async-done(((bf16[8,320,128]{2,1,0:T(8,128)(2,1)}), bf16[8,320,128]{2,1,0:T(8,128)(2,1)S(1)}, u32[]{:S(2)}, u32[]{:S(2)}) %all-to-all-start) | async-done | bytes 655392 | tf_op jit(solution)/shard_map/all_to_all | solution.py:659
  38.5 3.7 %collective-permute-start.1 = (bf16[160,256]{1,0:T(8,128)(2,1)}, bf16[160,256]{1,0:T(8,128)(2,1)S(1)}, u32[]{:S(2)}, u32[]{:S(2)}) collective-permute-start(bf16[160,256]{1,0:T(8,128)(2,1)} %spectrum.2), channel_id=1, source_target_pairs={{0,64},{8,72},{16,80},{24,88},{32,96},{40,104},{48,112},{56,120},{... | collective-permute-start | bytes 245768 | tf_op jit(solution)/shard_map/ppermute | solution.py:664
  53.8 4.2 %collective-permute-done.4.x_ref = bf16[160,256]{1,0:T(8,128)(2,1)S(1)} collective-permute-done((bf16[160,256]{1,0:T(8,128)(2,1)}, bf16[160,256]{1,0:T(8,128)(2,1)S(1)}, u32[]{:S(2)}, u32[]{:S(2)}) %collective-permute-start.4) | collective-permute-done | bytes 81952 | tf_op jit(solution)/shard_map/ppermute | solution.py:664
  58.0 4.6 %all-to-all-start.1 = ((bf16[8,160,128]{2,1,0:T(8,128)(2,1)}), bf16[8,160,128]{2,1,0:T(8,128)(2,1)S(1)}, u32[]{:S(2)}, u32[]{:S(2)}) async-start(bf16[8,160,128]{2,1,0:T(8,128)(2,1)} %mix_out.2), calls=%async_computation.1 | async-start | bytes 655360 | tf_op jit(solution)/shard_map/all_to_all | solution.py:659
  68.2 5.4 %collective-permute-start.6 = (bf16[10,2,64,512]{3,2,1,0:T(8,128)(2,1)}, bf16[10,2,64,512]{3,2,1,0:T(8,128)(2,1)S(1)}, u32[]{:S(2)}, u32[]{:S(2)}) collective-permute-start(bf16[10,2,64,512]{3,2,1,0:T(8,128)(2,1)} %bitcast.47), channel_id=1, source_target_pairs={{0,120},{8,0},{16,8},{24,16},{32,24},{40,32},{48,40},{56,48},{64,5... | collective-permute-start | bytes 3932168 | tf_op jit(solution)/shard_map/ppermute | solution.py:664
  73.6 9.1 %forward_rows.3 = (bf16[10,2,64,512]{3,2,1,0:T(8,128)(2,1)}, bf16[8,320,128]{2,1,0:T(8,128)(2,1)}, bf16[10,2,64,512]{3,2,1,0:T(8,128)(2,1)}, bf16[10,2,64,512]{3,2,1,0:T(8,128)(2,1)}) custom-call(bf16[5,2,64,512]{3,2,1,0:T(8,128)(2,1)} %copy-done.2, bf16[3,2,64,512]{3,2,1,0:T(8,128)(2,1)} %copy-done.4, ...), custom_call_target="tpu_custom_call", output_to_operand_aliasing={{1}: (9, {})} | custom-call | tf_op jit(solution)/shard_map/forward_rows/pallas_call | solution.py:467
  82.7 13.5 %all_to_all.40.recv_ref.refs_1_ = bf16[8,320,128]{2,1,0:T(8,128)(2,1)} all-to-all(bf16[8,320,128]{2,1,0:T(8,128)(2,1)} %get-tuple-element.85), channel_id=1, replica_groups=mesh['section'=16,'slab'=8] {'slab'}, dimensions={0} | all-to-all | bytes 1310720 | tf_op jit(solution)/shard_map/all_to_all | solution.py:659
  96.2 3.9 %modes.2 = (bf16[160,256]{1,0:T(8,128)(2,1)}, bf16[8,160,128]{2,1,0:T(8,128)(2,1)}) custom-call(bf16[8,320,128]{2,1,0:T(8,128)(2,1)} %all_to_all.40.recv_ref.refs_1_, bf16[2,8,800,128]{3,2,1,0:T(8,128)(2,1)} %bitcast.35, bf16[8,128,256]{2,1,0:T(8,128)(2,1)} %constant.14.clone.col_ref.refs_2_), custom_call_target="tpu_custom_call" | custom-call | tf_op jit(solution)/shard_map/modes/pallas_call | solution.py:467
  100.1 4.9 %all-to-all-start.3 = ((bf16[8,160,128]{2,1,0:T(8,128)(2,1)}), bf16[8,160,128]{2,1,0:T(8,128)(2,1)S(1)}, u32[]{:S(2)}, u32[]{:S(2)}) async-start(bf16[8,160,128]{2,1,0:T(8,128)(2,1)} %get-tuple-element.86), calls=%async_computation.3 | async-start | bytes 655360 | tf_op jit(solution)/shard_map/all_to_all | solution.py:659
  104.9 8.0 %forward_rows.4 = (bf16[10,2,64,512]{3,2,1,0:T(8,128)(2,1)}, bf16[8,320,128]{2,1,0:T(8,128)(2,1)}) custom-call(bf16[10,2,64,512]{3,2,1,0:T(8,128)(2,1)} %collective-permute-done.5.refs_0_, bf16[8,320,128]{2,1,0:T(8,128)(2,1)} %all_to_all.40.recv_ref.refs_1_, bf16[2,160,160]{2,1,0:T(8,128)(2,1)} %get-tuple-element.80.refs_4_.refs_2_.refs_9_, ...), custom_call_target="tpu_custom_call" | custom-call | tf_op jit(solution)/shard_map/forward_rows/pallas_call | solution.py:467
  114.1 15.3 %back_rows.2 = (bf16[10,2,64,512]{3,2,1,0:T(8,128)(2,1)}, bf16[8,320,128]{2,1,0:T(8,128)(2,1)}, f32[80,128]{1,0:T(8,128)}) custom-call(bf16[10,2,64,512]{3,2,1,0:T(8,128)(2,1)} %get-tuple-element.84.refs_0_, bf16[8,160,128]{2,1,0:T(8,128)(2,1)} %copy-done.6, ...), custom_call_target="tpu_custom_call", output_to_operand_aliasing={{1}: (10, {})} | custom-call | tf_op jit(solution)/shard_map/back_rows/pallas_call | solution.py:467
  129.4 15.1 %all_to_all.41.refs_0_.recv_ref = bf16[8,320,128]{2,1,0:T(8,128)(2,1)} all-to-all(bf16[8,320,128]{2,1,0:T(8,128)(2,1)} %get-tuple-element.96), channel_id=1, replica_groups=mesh['section'=16,'slab'=8] {'slab'}, dimensions={0} | all-to-all | bytes 1310720 | tf_op jit(solution)/shard_map/all_to_all | solution.py:659
  144.5 3.8 %modes_back.2 = (bf16[8,160,128]{2,1,0:T(8,128)(2,1)}, bf16[160,256]{1,0:T(8,128)(2,1)}) custom-call(bf16[8,320,128]{2,1,0:T(8,128)(2,1)} %all_to_all.41.refs_0_.recv_ref, bf16[2,8,800,128]{3,2,1,0:T(8,128)(2,1)} %bitcast.36, bf16[8,128,256]{2,1,0:T(8,128)(2,1)} %constant.14.clone.col_ref.refs_2_), custom_call_target="tpu_custom_call" | custom-call | tf_op jit(solution)/shard_map/modes_back/pallas_call | solution.py:467
  148.3 4.9 %all-to-all-start.5 = ((bf16[8,160,128]{2,1,0:T(8,128)(2,1)}), bf16[8,160,128]{2,1,0:T(8,128)(2,1)S(1)}, u32[]{:S(2)}, u32[]{:S(2)}) async-start(bf16[8,160,128]{2,1,0:T(8,128)(2,1)} %get-tuple-element.97), calls=%async_computation.5 | async-start | bytes 655360 | tf_op jit(solution)/shard_map/all_to_all | solution.py:659
  153.1 3.9 %modes.3 = (bf16[160,256]{1,0:T(8,128)(2,1)}, bf16[8,320,128]{2,1,0:T(8,128)(2,1)}) custom-call(bf16[8,320,128]{2,1,0:T(8,128)(2,1)} %all_to_all.41.refs_0_.recv_ref, bf16[2,8,800,128]{3,2,1,0:T(8,128)(2,1)} %bitcast.37, bf16[8,128,256]{2,1,0:T(8,128)(2,1)} %constant.14.clone.col_ref.refs_2_), custom_call_target="tpu_custom_call" | custom-call | tf_op jit(solution)/shard_map/modes/pallas_call | solution.py:467
  159.5 15.1 %back_rows.3 = (bf16[10,2,64,512]{3,2,1,0:T(8,128)(2,1)}, bf16[8,320,128]{2,1,0:T(8,128)(2,1)}, f32[80,128]{1,0:T(8,128)}) custom-call(bf16[5,2,64,512]{3,2,1,0:T(8,128)(2,1)} %copy-done.2, bf16[3,2,64,512]{3,2,1,0:T(8,128)(2,1)} %copy-done.4, bf16[2,2,64,512]{3,2,1,0:T(8,128)(2,1)} %copy-done.10, ...), custom_call_target="tpu_custom_call", output_to_operand_aliasing={{1}: (14, {})} | custom-call | tf_op jit(solution)/shard_map/back_rows/pallas_call | solution.py:467
  174.6 5.1 %all-to-all-start.6 = ((bf16[8,320,128]{2,1,0:T(8,128)(2,1)}), bf16[8,320,128]{2,1,0:T(8,128)(2,1)S(1)}, u32[]{:S(2)}, u32[]{:S(2)}) async-start(bf16[8,320,128]{2,1,0:T(8,128)(2,1)} %get-tuple-element.105), calls=%async_computation.6 | async-start | bytes 1310720 | tf_op jit(solution)/shard_map/all_to_all | solution.py:659
  182.5 4.6 %all-to-all-done.6.refs_0_.refs_1_ = bf16[8,320,128]{2,1,0:T(8,128)(2,1)S(1)} async-done(((bf16[8,320,128]{2,1,0:T(8,128)(2,1)}), bf16[8,320,128]{2,1,0:T(8,128)(2,1)S(1)}, u32[]{:S(2)}, u32[]{:S(2)}) %all-to-all-start.6) | async-done | bytes 655392 | tf_op jit(solution)/shard_map/all_to_all | solution.py:659
  188.0 3.9 %modes_back.3 = (bf16[8,240,128]{2,1,0:T(8,128)(2,1)}, bf16[160,256]{1,0:T(8,128)(2,1)}) custom-call(bf16[8,320,128]{2,1,0:T(8,128)(2,1)} %copy-done, bf16[2,8,800,128]{3,2,1,0:T(8,128)(2,1)} %bitcast.38, bf16[8,128,256]{2,1,0:T(8,128)(2,1)} %constant.14.clone.col_ref.refs_2_, f32[80,128]{1,0:T(8,128)} %get-tuple-element.109.refs_3_), custom_call_target="tpu_custom_call" | custom-call | tf_op jit(solution)/shard_map/modes_back/pallas_call | solution.py:467
  191.8 4.8 %all-to-all-start.7 = ((bf16[8,240,128]{2,1,0:T(8,128)(2,1)}), bf16[8,240,128]{2,1,0:T(8,128)(2,1)S(1)}, u32[]{:S(2)}, u32[]{:S(2)}) async-start(bf16[8,240,128]{2,1,0:T(8,128)(2,1)} %get-tuple-element.110), calls=%async_computation.7 | async-start | bytes 983040 | tf_op jit(solution)/shard_map/all_to_all | solution.py:659
  196.7 7.7 %forward_rows.5 = bf16[10,2,64,512]{3,2,1,0:T(8,128)(2,1)} custom-call(bf16[10,2,64,512]{3,2,1,0:T(8,128)(2,1)} %get-tuple-element.113.refs_0_, bf16[8,320,128]{2,1,0:T(8,128)(2,1)} %copy-done, bf16[2,160,160]{2,1,0:T(8,128)(2,1)} %get-tuple-element.80.refs_4_.refs_2_.refs_9_, bf16[2,640,160]{2,1,0:T(8,128)(2,1)} %get-tuple-element.81.refs_5_.refs_3_.refs_4_.refs_6_, ...), custom_call_target="tpu_custom_call" | custom-call | tf_op jit(solution)/shard_map/forward_rows/pallas_call | solution.py:467
  (61 shorter events, 50.2 us)
Async XLA Ops:
  0.6 6.2 %copy-start.13 = (bf16[1,2,20,20]{3,1,2,0:T(2,128)(2,1)S(1)}, bf16[1,2,20,20]{3,1,2,0:T(2,128)(2,1)}, u32[]{:S(2)}) copy-start(bf16[1,2,20,20]{3,1,2,0:T(2,128)(2,1)} %param.15) | copy-start | bytes 4804
  0.6 6.8 %copy-start.14 = (bf16[1,2,20,80]{3,1,2,0:T(2,128)(2,1)S(1)}, bf16[1,2,20,80]{3,1,2,0:T(2,128)(2,1)}, u32[]{:S(2)}) copy-start(bf16[1,2,20,80]{3,1,2,0:T(2,128)(2,1)} %param.17) | copy-start | bytes 19204
  0.7 7.4 %copy-start.15 = (bf16[1,2,80,20]{2,1,3,0:T(2,128)(2,1)S(1)}, bf16[1,2,80,20]{2,1,3,0:T(2,128)(2,1)}, u32[]{:S(2)}) copy-start(bf16[1,2,80,20]{2,1,3,0:T(2,128)(2,1)} %param.16) | copy-start | bytes 19204
  1.8 18.7 %collective-permute-start = (bf16[5,2,64,512]{3,2,1,0:T(8,128)(2,1)S(1)}, bf16[5,2,64,512]{3,2,1,0:T(8,128)(2,1)S(1)}, u32[]{:S(2)}, u32[]{:S(2)}) collective-permute-start(bf16[5,2,64,512]{3,2,1,0:T(8,128)(2,1)S(1)} %bitcast.44), channel_id=1, source_target_pairs={{0,64},{8,72},{16,80},{24,88},{32,96},{40,104},{48,112},{56,120},{... | collective-permute-start | bytes 1966088 | tf_op jit(solution)/shard_map/ppermute | solution.py:664
  20.5 22.6 %copy-start.2 = (bf16[5,2,64,512]{3,2,1,0:T(8,128)(2,1)}, bf16[5,2,64,512]{3,2,1,0:T(8,128)(2,1)S(1)}, u32[]{:S(2)}) copy-start(bf16[5,2,64,512]{3,2,1,0:T(8,128)(2,1)S(1)} %collective-permute-done.refs_0_) | copy-start | bytes 1966084
  20.5 15.1 %all-to-all-start = ((bf16[8,320,128]{2,1,0:T(8,128)(2,1)}), bf16[8,320,128]{2,1,0:T(8,128)(2,1)S(1)}, u32[]{:S(2)}, u32[]{:S(2)}) async-start(bf16[8,320,128]{2,1,0:T(8,128)(2,1)} %row_dft.3), calls=%async_computation | async-start | bytes 1310720 | tf_op jit(solution)/shard_map/all_to_all | solution.py:659
  26.1 18.8 %collective-permute-start.2 = (bf16[3,2,64,512]{3,2,1,0:T(8,128)(2,1)S(1)}, bf16[3,2,64,512]{3,2,1,0:T(8,128)(2,1)S(1)}, u32[]{:S(2)}, u32[]{:S(2)}) collective-permute-start(bf16[3,2,64,512]{3,2,1,0:T(8,128)(2,1)S(1)} %bitcast.45), channel_id=1, source_target_pairs={{0,64},{8,72},{16,80},{24,88},{32,96},{40,104},{48,112},{56,120},{... | collective-permute-start | bytes 1179656 | tf_op jit(solution)/shard_map/ppermute | solution.py:664
  38.5 7.6 %collective-permute-start.1 = (bf16[160,256]{1,0:T(8,128)(2,1)}, bf16[160,256]{1,0:T(8,128)(2,1)S(1)}, u32[]{:S(2)}, u32[]{:S(2)}) collective-permute-start(bf16[160,256]{1,0:T(8,128)(2,1)} %spectrum.2), channel_id=1, source_target_pairs={{0,64},{8,72},{16,80},{24,88},{32,96},{40,104},{48,112},{56,120},{... | collective-permute-start | bytes 245768 | tf_op jit(solution)/shard_map/ppermute | solution.py:664
  44.9 8.9 %copy-start.4 = (bf16[3,2,64,512]{3,2,1,0:T(8,128)(2,1)}, bf16[3,2,64,512]{3,2,1,0:T(8,128)(2,1)S(1)}, u32[]{:S(2)}) copy-start(bf16[3,2,64,512]{3,2,1,0:T(8,128)(2,1)S(1)} %collective-permute-done.2.refs_1_) | copy-start | bytes 1179652
  46.0 4.3 %copy-start.11 = (bf16[160,256]{1,0:T(8,128)(2,1)}, bf16[160,256]{1,0:T(8,128)(2,1)S(1)}, u32[]{:S(2)}) copy-start(bf16[160,256]{1,0:T(8,128)(2,1)S(1)} %collective-permute-done.1.x_ref) | copy-start | bytes 245764
  46.0 12.0 %collective-permute-start.3 = (bf16[2,2,64,512]{3,2,1,0:T(8,128)(2,1)S(1)}, bf16[2,2,64,512]{3,2,1,0:T(8,128)(2,1)S(1)}, u32[]{:S(2)}, u32[]{:S(2)}) collective-permute-start(bf16[2,2,64,512]{3,2,1,0:T(8,128)(2,1)S(1)} %bitcast.46), channel_id=1, source_target_pairs={{0,64},{8,72},{16,80},{24,88},{32,96},{40,104},{48,112},{56,120},{... | collective-permute-start | bytes 786440 | tf_op jit(solution)/shard_map/ppermute | solution.py:664
  50.3 7.7 %collective-permute-start.4 = (bf16[160,256]{1,0:T(8,128)(2,1)}, bf16[160,256]{1,0:T(8,128)(2,1)S(1)}, u32[]{:S(2)}, u32[]{:S(2)}) collective-permute-start(bf16[160,256]{1,0:T(8,128)(2,1)} %spectrum.3), channel_id=1, source_target_pairs={{0,8},{8,16},{16,24},{24,32},{32,40},{40,48},{48,56},{56,64},{64,7... | collective-permute-start | bytes 245768 | tf_op jit(solution)/shard_map/ppermute | solution.py:664
  58.0 4.6 %copy-start.12 = (bf16[160,256]{1,0:T(8,128)(2,1)}, bf16[160,256]{1,0:T(8,128)(2,1)S(1)}, u32[]{:S(2)}) copy-start(bf16[160,256]{1,0:T(8,128)(2,1)S(1)} %collective-permute-done.4.x_ref) | copy-start | bytes 245764
  58.0 8.2 %copy-start.10 = (bf16[2,2,64,512]{3,2,1,0:T(8,128)(2,1)}, bf16[2,2,64,512]{3,2,1,0:T(8,128)(2,1)S(1)}, u32[]{:S(2)}) copy-start(bf16[2,2,64,512]{3,2,1,0:T(8,128)(2,1)S(1)} %collective-permute-done.3.refs_2_) | copy-start | bytes 786436
  58.0 10.2 %all-to-all-start.1 = ((bf16[8,160,128]{2,1,0:T(8,128)(2,1)}), bf16[8,160,128]{2,1,0:T(8,128)(2,1)S(1)}, u32[]{:S(2)}, u32[]{:S(2)}) async-start(bf16[8,160,128]{2,1,0:T(8,128)(2,1)} %mix_out.2), calls=%async_computation.1 | async-start | bytes 655360 | tf_op jit(solution)/shard_map/all_to_all | solution.py:659
  62.6 5.6 %copy-start.8 = (bf16[1,20,64,512]{3,2,1,0:T(8,128)(2,1)S(1)}, bf16[1,20,64,512]{3,2,1,0:T(8,128)(2,1)}, u32[]{:S(2)}) copy-start(bf16[1,20,64,512]{3,2,1,0:T(8,128)(2,1)} %param.12) | copy-start | bytes 3932164
  68.2 5.4 %copy-start.7 = (bf16[8,160,128]{2,1,0:T(8,128)(2,1)}, bf16[8,160,128]{2,1,0:T(8,128)(2,1)S(1)}, u32[]{:S(2)}) copy-start(bf16[8,160,128]{2,1,0:T(8,128)(2,1)S(1)} %all-to-all-done.1.refs_3_) | copy-start | bytes 983044
  68.2 36.7 %collective-permute-start.5 = (bf16[10,2,64,512]{3,2,1,0:T(8,128)(2,1)S(1)}, bf16[10,2,64,512]{3,2,1,0:T(8,128)(2,1)}, u32[]{:S(2)}, u32[]{:S(2)}) collective-permute-start(bf16[10,2,64,512]{3,2,1,0:T(8,128)(2,1)S(1)} %bitcast.43), channel_id=1, source_target_pairs={{0,8},{8,16},{16,24},{24,32},{32,40},{40,48},{48,56},{56,64},{64,7... | collective-permute-start | bytes 3932168 | tf_op jit(solution)/shard_map/ppermute | solution.py:664
  68.2 44.7 %collective-permute-start.6 = (bf16[10,2,64,512]{3,2,1,0:T(8,128)(2,1)}, bf16[10,2,64,512]{3,2,1,0:T(8,128)(2,1)S(1)}, u32[]{:S(2)}, u32[]{:S(2)}) collective-permute-start(bf16[10,2,64,512]{3,2,1,0:T(8,128)(2,1)} %bitcast.47), channel_id=1, source_target_pairs={{0,120},{8,0},{16,8},{24,16},{32,24},{40,32},{48,40},{56,48},{64,5... | collective-permute-start | bytes 3932168 | tf_op jit(solution)/shard_map/ppermute | solution.py:664
  100.1 12.9 %all-to-all-start.3 = ((bf16[8,160,128]{2,1,0:T(8,128)(2,1)}), bf16[8,160,128]{2,1,0:T(8,128)(2,1)S(1)}, u32[]{:S(2)}, u32[]{:S(2)}) async-start(bf16[8,160,128]{2,1,0:T(8,128)(2,1)} %get-tuple-element.86), calls=%async_computation.3 | async-start | bytes 655360 | tf_op jit(solution)/shard_map/all_to_all | solution.py:659
  112.9 1.2 copy-start.9
  148.3 10.5 %all-to-all-start.5 = ((bf16[8,160,128]{2,1,0:T(8,128)(2,1)}), bf16[8,160,128]{2,1,0:T(8,128)(2,1)S(1)}, u32[]{:S(2)}, u32[]{:S(2)}) async-start(bf16[8,160,128]{2,1,0:T(8,128)(2,1)} %get-tuple-element.97), calls=%async_computation.5 | async-start | bytes 655360 | tf_op jit(solution)/shard_map/all_to_all | solution.py:659
  174.6 12.6 %all-to-all-start.6 = ((bf16[8,320,128]{2,1,0:T(8,128)(2,1)}), bf16[8,320,128]{2,1,0:T(8,128)(2,1)S(1)}, u32[]{:S(2)}, u32[]{:S(2)}) async-start(bf16[8,320,128]{2,1,0:T(8,128)(2,1)} %get-tuple-element.105), calls=%async_computation.6 | async-start | bytes 1310720 | tf_op jit(solution)/shard_map/all_to_all | solution.py:659
  191.8 15.4 %all-to-all-start.7 = ((bf16[8,240,128]{2,1,0:T(8,128)(2,1)}), bf16[8,240,128]{2,1,0:T(8,128)(2,1)S(1)}, u32[]{:S(2)}, u32[]{:S(2)}) async-start(bf16[8,240,128]{2,1,0:T(8,128)(2,1)} %get-tuple-element.110), calls=%async_computation.7 | async-start | bytes 983040 | tf_op jit(solution)/shard_map/all_to_all | solution.py:659
  (5 other events, 4.0 us)
